TPU v7x, 128 devices: a whole 4x4x4 slice. The times are simulated.
128 devices in a mesh: row: 8 (over z, x_lo), col: 16 (over x_hi, y, core).
Axes of the slice: x: 4 (x_hi: 2, x_lo: 2; x = x_hi * 2 + x_lo), y: 4, z: 4, core: 2. Of those that a mesh axis runs over, the one named last changes fastest.
Arguments:
- blocks: bfloat16 [8, 16, 192, 128, 128], P('row', 'col'), may hold values from -0.059814453 to 0.059814453
- block_rows: int32 [8, 16, 192], P('row', 'col'), may hold values from 0 to 255, as said below
- block_cols: int32 [8, 16, 192], P('row', 'col'), may hold values from 0 to 255, as said below
- counts: int32 [8, 16], P('row', 'col'), may hold values from 96 to 192, as said below
- travel_times: float32 [16, 262144], P(None, ('row', 'col')), may hold values from -6 to 6
Outputs:
- solution: float32 [16, 16, 8, 4096], P(None, 'col', 'row')
- scaled_direction: float32 [16, 16, 8, 4096], P(None, 'col', 'row')
Inputs may be any that keep to these rules, and one draw needn't show every extreme that they name: Ray block of a slot within the 256 ray blocks of its row group; among the filled slots of one device the (block_rows, block_cols) pairs are all different. `block_cols`: cell block of a slot within the 256 cell blocks of its column group. `counts`: some device fills all 192 slots.
All inputs are finite; a program needn't handle non-finite values.
Results may differ from a plain program's by a relative error of at most 0.0054.
Values may be sent and summed in bfloat16 or wider, within the bound.
No kernel may reach another device: no remote copies, remote signals or barrier semaphores. Data moves between devices by JAX's collectives and lax.ppermute only.
A program may use at most 64 MiB of HBM per device.

v0:
```python
import jax
import jax.numpy as jnp
from jax import lax
from jax.sharding import PartitionSpec as P

RB_DEV = 256
CB_DEV = 256
ITERS = 2


norm_eps = 1e-06


def rotation(rho_bar, phi_bar, beta_norm, alpha_norm):
    rho_new = jnp.sqrt(rho_bar * rho_bar + beta_norm * beta_norm)
    cosine = rho_bar / rho_new
    sine_val = beta_norm / rho_new
    theta_coef = sine_val * alpha_norm
    rho_next = -cosine * alpha_norm
    phi_new = cosine * phi_bar
    phi_next = sine_val * phi_bar
    return (phi_new / rho_new, theta_coef / rho_new, rho_next, phi_next)


def forward_rows(right_full, blocks_here, cols_here, row_hot):
    count_rhs = right_full.shape[0]
    block_size = blocks_here.shape[1]
    cells = right_full.reshape(count_rhs, right_full.shape[1] // block_size, block_size)
    picked = jnp.take(cells, cols_here, axis=1)
    product = jnp.einsum("knj,nij->kni", picked, blocks_here, preferred_element_type=jnp.float32)
    summed = jnp.einsum("rn,kni->kri", row_hot, product, precision=lax.Precision.HIGHEST)
    return summed.reshape(count_rhs, -1)


def backward_cols(left_full, blocks_here, rows_here, col_hot):
    count_rhs = left_full.shape[0]
    block_size = blocks_here.shape[1]
    rays = left_full.reshape(count_rhs, left_full.shape[1] // block_size, block_size)
    picked = jnp.take(rays, rows_here, axis=1)
    product = jnp.einsum("kni,nij->knj", picked, blocks_here, preferred_element_type=jnp.float32)
    summed = jnp.einsum("cn,knj->kcj", col_hot, product, precision=lax.Precision.HIGHEST)
    return summed.reshape(count_rhs, -1)


def square_sums(values):
    return jnp.sum(values * values, axis=1)


def shards(blocks, block_rows, block_cols, counts, travel_times):
    blocks_here = blocks[0, 0]
    rows_here = block_rows[0, 0]
    cols_here = block_cols[0, 0]
    slots = jnp.arange(blocks_here.shape[0], dtype=jnp.int32)
    filled = slots < counts[0, 0]
    row_hot = (
        (rows_here[None, :] == jnp.arange(RB_DEV, dtype=jnp.int32)[:, None]) & filled[None, :]
    ).astype(jnp.float32)
    col_hot = (
        (cols_here[None, :] == jnp.arange(CB_DEV, dtype=jnp.int32)[:, None]) & filled[None, :]
    ).astype(jnp.float32)
    count_rhs = travel_times.shape[0]

    def global_norm(partial_value):
        return jnp.sqrt(lax.psum(square_sums(partial_value), ("row", "col")) + norm_eps)

    def ray_side(partial_value):
        beta_norm = global_norm(partial_value)
        left_full = lax.all_gather(
            (partial_value / beta_norm[:, None]).astype(jnp.bfloat16), "col", axis=1, tiled=True
        )
        return (partial_value / beta_norm[:, None], left_full, beta_norm)

    def cell_side(partial_value):
        alpha_norm = global_norm(partial_value)
        right_full = None
        return (partial_value / alpha_norm[:, None], right_full, alpha_norm)

    def rows_to_cells(left_full):
        partial_value = backward_cols(left_full, blocks_here, rows_here, col_hot)
        return lax.psum_scatter(partial_value, "row", scatter_dimension=1, tiled=True)

    left_vec, left_full, beta_norm = ray_side(travel_times)
    right_vec, right_full, alpha_norm = cell_side(rows_to_cells(left_full))
    direction = right_vec
    solution = jnp.zeros_like(right_vec)
    phi_bar = beta_norm
    rho_bar = alpha_norm
    for iteration in range(ITERS):
        cells_right_full = lax.all_gather(right_vec.astype(jnp.bfloat16), "row", axis=1, tiled=True)
        cells_partial_value = forward_rows(cells_right_full, blocks_here, cols_here, row_hot)
        left_vec, left_full, beta_norm = ray_side(
            lax.psum_scatter(cells_partial_value, "col", scatter_dimension=1, tiled=True)
            - alpha_norm[:, None] * left_vec
        )
        right_vec, right_full, alpha_norm = cell_side(
            rows_to_cells(left_full) - beta_norm[:, None] * right_vec
        )
        step_scale, turn_scale, rho_bar, phi_bar = rotation(rho_bar, phi_bar, beta_norm, alpha_norm)
        solution = solution + step_scale[:, None] * direction
        direction = right_vec - turn_scale[:, None] * direction
    scaled = phi_bar[:, None] * direction
    return (solution.reshape(count_rhs, 1, 1, -1), scaled.reshape(count_rhs, 1, 1, -1))


def solution(mesh):
    placed = (
        P("row", "col", None, None, None),
        P("row", "col", None),
        P("row", "col", None),
        P("row", "col"),
        P(None, ("row", "col")),
    )
    return jax.shard_map(
        shards,
        mesh=mesh,
        in_specs=placed,
        out_specs=(P(None, "col", "row", None), P(None, "col", "row", None)),
        check_vma=False,
    )
```

profile of v0, /device:TPU:0, one launch (start us, length us, event | category | flops | bytes accessed | tf_op | source)
XLA Modules:
  0.0 989.3 jit_solution(17914631215639586107)
XLA Ops:
  8.2 68.2 %psum.42 = f32[16]{0:T(128)S(1)} all-reduce(f32[16]{0:T(128)S(1)} %multiply_reduce_fusion.5), channel_id=1, replica_groups=mesh['row'=8,'col'=16] {'row','col'}, use_global_device_ids=true, to_apply=%region_1.0 | all-reduce | flops 16 | bytes 128 | tf_op jit(solution)/shard_map/psum | solution.py:64
  80.2 38.8 %all-gather.6.cloned.1.call-done = bf16[16,32768]{1,0:T(8,128)(2,1)} async-done(((bf16[16,2048]{1,0:T(8,128)(2,1)}), bf16[16,32768]{1,0:T(8,128)(2,1)}) %all-gather.6.cloned.1.call-update) | async-done | bytes 1048592 | tf_op jit(solution)/shard_map/all_gather | solution.py:68
  121.2 3.9 fusion.15
  125.2 2.0 convolution_bitcast_fusion.4
  127.2 1.8 copy.16
  129.0 4.2 copy.65
  133.2 51.8 %reduce-scatter.6.cloned.1.call-done = f32[16,4096]{1,0:T(8,128)} async-done(((f32[16,32768]{1,0:T(8,128)}), f32[16,4096]{1,0:T(8,128)}) %reduce-scatter.6.cloned.1.call-update) | async-done | bytes 262160 | tf_op jit(solution)/shard_map/reduce_scatter | solution.py:80
  186.1 64.3 %psum.43 = f32[16]{0:T(128)S(1)} all-reduce(f32[16]{0:T(128)S(1)} %multiply_reduce_fusion.2), channel_id=1, replica_groups=mesh['row'=8,'col'=16] {'row','col'}, use_global_device_ids=true, to_apply=%region_4.6 | all-reduce | flops 16 | bytes 128 | tf_op jit(solution)/shard_map/psum | solution.py:64
  252.4 37.8 %all-gather.8.cloned.1.call-done = bf16[16,32768]{1,0:T(8,128)(2,1)} async-done(((bf16[16,4096]{1,0:T(8,128)(2,1)}), bf16[16,32768]{1,0:T(8,128)(2,1)}) %all-gather.8.cloned.1.call-update) | async-done | bytes 1048592 | tf_op jit(solution)/shard_map/all_gather | solution.py:89
  292.4 5.5 fusion.18
  297.9 2.0 convolution_bitcast_fusion.3
  301.7 4.2 copy.64
  305.9 69.8 %reduce-scatter.8.cloned.1.call-done = f32[16,2048]{1,0:T(8,128)} async-done(((f32[16,32768]{1,0:T(8,128)}), f32[16,2048]{1,0:T(8,128)}) %reduce-scatter.8.cloned.1.call-update) | async-done | bytes 131088 | tf_op jit(solution)/shard_map/reduce_scatter | solution.py:92
  376.9 64.7 %psum.44 = f32[16]{0:T(128)S(1)} all-reduce(f32[16]{0:T(128)S(1)} %get-tuple-element.17), channel_id=1, replica_groups=mesh['row'=8,'col'=16] {'row','col'}, use_global_device_ids=true, to_apply=%region_7.9 | all-reduce | flops 16 | bytes 128 | tf_op jit(solution)/shard_map/psum | solution.py:64
  442.4 40.9 %all-gather.10.cloned.1.call-done = bf16[16,32768]{1,0:T(8,128)(2,1)} async-done(((bf16[16,2048]{1,0:T(8,128)(2,1)}), bf16[16,32768]{1,0:T(8,128)(2,1)}) %all-gather.10.cloned.1.call-update) | async-done | bytes 1048592 | tf_op jit(solution)/shard_map/all_gather | solution.py:68
  485.5 3.9 fusion.21
  489.4 2.0 convolution_bitcast_fusion.2
  493.2 4.2 copy.63
  497.5 51.8 %reduce-scatter.10.cloned.1.call-done = f32[16,4096]{1,0:T(8,128)} async-done(((f32[16,32768]{1,0:T(8,128)}), f32[16,4096]{1,0:T(8,128)}) %reduce-scatter.10.cloned.1.call-update) | async-done | bytes 262160 | tf_op jit(solution)/shard_map/reduce_scatter | solution.py:80
  550.4 64.5 %psum.45 = f32[16]{0:T(128)S(1)} all-reduce(f32[16]{0:T(128)S(1)} %multiply_reduce_fusion.1), channel_id=1, replica_groups=mesh['row'=8,'col'=16] {'row','col'}, use_global_device_ids=true, to_apply=%region_10.12 | all-reduce | flops 16 | bytes 128 | tf_op jit(solution)/shard_map/psum | solution.py:64
  616.8 38.0 %all-gather.12.cloned.1.call-done = bf16[16,32768]{1,0:T(8,128)(2,1)} async-done(((bf16[16,4096]{1,0:T(8,128)(2,1)}), bf16[16,32768]{1,0:T(8,128)(2,1)}) %all-gather.12.cloned.1.call-update) | async-done | bytes 1048592 | tf_op jit(solution)/shard_map/all_gather | solution.py:89
  656.9 5.5 fusion.24
  662.4 2.0 convolution_bitcast_fusion.1
  666.3 4.2 copy.62
  670.5 69.8 %reduce-scatter.12.cloned.1.call-done = f32[16,2048]{1,0:T(8,128)} async-done(((f32[16,32768]{1,0:T(8,128)}), f32[16,2048]{1,0:T(8,128)}) %reduce-scatter.12.cloned.1.call-update) | async-done | bytes 131088 | tf_op jit(solution)/shard_map/reduce_scatter | solution.py:92
  741.5 64.7 %psum.46 = f32[16]{0:T(128)S(1)} all-reduce(f32[16]{0:T(128)S(1)} %get-tuple-element.13), channel_id=1, replica_groups=mesh['row'=8,'col'=16] {'row','col'}, use_global_device_ids=true, to_apply=%region_13.15 | all-reduce | flops 16 | bytes 128 | tf_op jit(solution)/shard_map/psum | solution.py:64
  807.3 40.6 %all-gather.14.cloned.1.call-done = bf16[16,32768]{1,0:T(8,128)(2,1)} async-done(((bf16[16,2048]{1,0:T(8,128)(2,1)}), bf16[16,32768]{1,0:T(8,128)(2,1)}) %all-gather.14.cloned.1.call-update) | async-done | bytes 1048592 | tf_op jit(solution)/shard_map/all_gather | solution.py:68
  850.1 3.9 fusion.27
  854.0 2.0 convolution_bitcast_fusion
  857.8 4.2 copy.61
  862.0 51.8 %reduce-scatter.14.cloned.1.call-done = f32[16,4096]{1,0:T(8,128)} async-done(((f32[16,32768]{1,0:T(8,128)}), f32[16,4096]{1,0:T(8,128)}) %reduce-scatter.14.cloned.1.call-update) | async-done | bytes 262160 | tf_op jit(solution)/shard_map/reduce_scatter | solution.py:80
  915.0 64.3 %psum.47 = f32[16]{0:T(128)S(1)} all-reduce(f32[16]{0:T(128)S(1)} %multiply_reduce_fusion), channel_id=1, replica_groups=mesh['row'=8,'col'=16] {'row','col'}, use_global_device_ids=true, to_apply=%region_16.18 | all-reduce | flops 16 | bytes 128 | tf_op jit(solution)/shard_map/psum | solution.py:64
  (69 shorter events, 37.0 us)
Async XLA Ops:
  7.2 111.9 %all-gather.6.cloned.1.call-start = ((), (), s32[]{:S(2)}) async-start(), calls=%async_computation.5 | async-start | bytes 1114112 | tf_op jit(solution)/shard_map/all_gather | solution.py:68
  78.1 106.9 %reduce-scatter.6.cloned.1.call-start = ((), (), s32[]{:S(2)}) async-start(), calls=%async_computation.6 | async-start | bytes 2359296 | tf_op jit(solution)/shard_map/reduce_scatter | solution.py:80
  121.2 3.9 copy-start.2
  133.2 157.0 %all-gather.8.cloned.1.call-start = ((), (), s32[]{:S(2)}) async-start(), calls=%async_computation.7 | async-start | bytes 1179648 | tf_op jit(solution)/shard_map/all_gather | solution.py:89
  252.1 123.6 %reduce-scatter.8.cloned.1.call-start = ((), (), s32[]{:S(2)}) async-start(), calls=%async_computation.8 | async-start | bytes 2228224 | tf_op jit(solution)/shard_map/reduce_scatter | solution.py:92
  292.4 5.5 copy-start.3
  305.9 69.9 %copy-start.1 = (f32[16,2048]{1,0:T(8,128)S(1)}, f32[16,2048]{1,0:T(8,128)}, u32[]{:S(2)}) copy-start(f32[16,2048]{1,0:T(8,128)} %param.11) | copy-start | bytes 393220
  305.9 177.4 %all-gather.10.cloned.1.call-start = ((), (), s32[]{:S(2)}) async-start(), calls=%async_computation.9 | async-start | bytes 1114112 | tf_op jit(solution)/shard_map/all_gather | solution.py:68
  442.4 106.9 %reduce-scatter.10.cloned.1.call-start = ((), (), s32[]{:S(2)}) async-start(), calls=%async_computation.10 | async-start | bytes 2359296 | tf_op jit(solution)/shard_map/reduce_scatter | solution.py:80
  497.4 51.9 %copy-start = (f32[16,4096]{1,0:T(8,128)S(1)}, f32[16,4096]{1,0:T(8,128)}, u32[]{:S(2)}) copy-start(f32[16,4096]{1,0:T(8,128)} %reduce-scatter.6.cloned.1.call-done) | copy-start | bytes 786436
  497.4 157.3 %all-gather.12.cloned.1.call-start = ((), (), s32[]{:S(2)}) async-start(), calls=%async_computation.11 | async-start | bytes 1179648 | tf_op jit(solution)/shard_map/all_gather | solution.py:89
  616.7 123.6 %reduce-scatter.12.cloned.1.call-start = ((), (), s32[]{:S(2)}) async-start(), calls=%async_computation.12 | async-start | bytes 2228224 | tf_op jit(solution)/shard_map/reduce_scatter | solution.py:92
  670.4 177.5 %all-gather.14.cloned.1.call-start = ((), (), s32[]{:S(2)}) async-start(), calls=%async_computation.13 | async-start | bytes 1114112 | tf_op jit(solution)/shard_map/all_gather | solution.py:68
  807.0 106.9 %reduce-scatter.14.cloned.1.call-start = ((), (), s32[]{:S(2)}) async-start(), calls=%async_computation.14 | async-start | bytes 2359296 | tf_op jit(solution)/shard_map/reduce_scatter | solution.py:80
Sparse Core Ops, SparseCore 0:
  78.2 40.7 all-gather.5
  133.3 51.6 reduce-scatter.5
  252.3 37.8 all-gather.7
  306.0 69.7 reduce-scatter.7
  442.5 40.7 all-gather.9
  497.5 51.6 reduce-scatter.9
  616.8 37.8 all-gather.11
  670.6 69.7 reduce-scatter.11
  807.1 40.7 all-gather.13
  862.1 51.6 reduce-scatter.13
where the time goes:
time: 991 us; the launch traced here: 989 us
  waiting for transfers between devices  491 us (50%)
  blocking collectives  391 us (39%)
  local copies, waits for them, and re-layouts  42.8 us (4%)
  matrix products  32.6 us (3%)
  other arithmetic  15.8 us (2%)
  between operations  15 us (2%)
    psum x6, blocking collectives, global_norm(): lax.psum(square_sums(partial_value), ('row', 'col')) + norm_eps  391 us
    reduce_scatter x3, waiting for transfers between devices, rows_to_cells(): lax.psum_scatter(partial_value, 'row', scatter_dimension=1, tiled=True)  155 us
    reduce_scatter x2, waiting for transfers between devices, shards(): lax.psum_scatter(cells_partial_value, 'col', scatter_dimension=1, tiled=T...  140 us
    all_gather x3, waiting for transfers between devices, ray_side(): lax.all_gather((partial_value / beta_norm[:, None]).astype(jnp.bfloat16),...  120 us
    all_gather x2, waiting for transfers between devices, shards(): lax.all_gather(right_vec.astype(jnp.bfloat16), 'row', axis=1, tiled=True)  75.7 us
    unnamed x15, local copies, waits for them, and re-layouts  22.8 us
  transfers between devices with their start and end apart: 10, of which 10 were waited for; matrix products, arithmetic and copies ran while one was open for 0% of the time, Pallas kernels for 0%

commit v1 on v0

v1 whole, which is shorter than its diff:
```python
import functools

import jax
import jax.numpy as jnp
from jax import lax
from jax.experimental import pallas as pl
from jax.experimental.pallas import tpu as pltpu
from jax.sharding import Mesh, PartitionSpec as P

ITERS = 2
LANES = 128
NORM_EPS = 1e-06
SQUARES_FLOOR = 1e-30
CELL_GAIN = 4096.0
RAY_GAIN = 2048.0
CHUNK = 16
CHIPS_OF_COL = ("xh", "y")
DEVICES_OF_ROW = ("z", "xl")
VMEM_BYTES = 24 << 20


def exponent_of(squares):
    return jnp.ceil(jnp.log2(jnp.maximum(squares, SQUARES_FLOOR)))


def side_lanes(lane, first, second, third):
    return jnp.where(lane == 0, first, jnp.where(lane == 1, second, jnp.where(lane == 2, third, 0.0)))


def side_of_squares(squares, lane):
    exponent = exponent_of(squares)
    fraction = squares * jnp.exp2(-exponent)
    upper = jnp.floor(fraction * 1024.0)
    return side_lanes(lane, exponent, upper, fraction * 1024.0 - upper), exponent


def squares_of_side(side):
    exponent = side[:, :, 0]
    return exponent, (side[:, :, 1] + side[:, :, 2]) * (1.0 / 1024.0) * jnp.exp2(exponent)


def fetch(chunk, blocks_hbm, held, sems):
    piece = pl.ds(chunk * CHUNK, CHUNK)
    return pltpu.make_async_copy(blocks_hbm.at[piece], held.at[piece], sems.at[chunk])


def products(count, blocks_hbm, held, sems, prepare, step):
    chunks = (count + (CHUNK - 1)) // CHUNK

    def begin(chunk, carry):
        fetch(chunk, blocks_hbm, held, sems).start()
        return carry

    def visit(chunk, carry):
        fetch(chunk, blocks_hbm, held, sems).wait()
        for at in range(CHUNK):
            step(chunk * CHUNK + at)
        return carry

    lax.fori_loop(0, chunks, begin, 0)
    prepare()
    lax.fori_loop(0, chunks, visit, 0)


def rays_kernel(rows, cols, scalars, right, blocks_hbm, keep, send, total, held, sems):
    count, core = scalars[0], scalars[1]
    half = keep.shape[0]

    def prepare():
        total[...] = jnp.zeros_like(total)
        side = sum(right[33 * at + 32].astype(jnp.float32) for at in range(8))
        squares = jnp.broadcast_to(jnp.sum(side, axis=1, keepdims=True), side.shape)
        for at in range(16):
            total[17 * at + 16] = squares

    def step(slot):
        row, col = rows[slot], cols[slot]
        picked = right[col + (col >> 5)]
        product = lax.dot_general(
            picked, held[slot], (((1,), (1,)), ((), ())), preferred_element_type=jnp.float32
        )
        place = (((row >> 4) & 1) ^ core) * half + (row >> 5) * 17 + (row & 15)
        total[place] += jnp.where(slot < count, product, 0.0)

    products(count, blocks_hbm, held, sems, prepare, step)
    keep[...] = total[:half]
    send[...] = total[half:]


def cells_kernel(rows, cols, scalars, left_own, left_other, blocks_hbm, out, left, held, sems):
    count, core = scalars[0], scalars[1]
    half = left_own.shape[0]
    left[pl.ds(core * half, half)] = left_own[...]
    left[pl.ds((1 - core) * half, half)] = left_other[...]
    side = sum(left[17 * at + 16].astype(jnp.float32) for at in range(16))
    squares = jnp.broadcast_to(jnp.sum(side, axis=1, keepdims=True), side.shape)
    lane = lax.broadcasted_iota(jnp.int32, side.shape, 1)
    packed, exponent = side_of_squares(squares, lane)
    scale = CELL_GAIN * jnp.exp2(-0.5 * exponent)

    def prepare():
        out[...] = jnp.zeros_like(out)
        for at in range(8):
            out[33 * at + 32] = packed

    def step(slot):
        row, col = rows[slot], cols[slot]
        picked = left[((row >> 4) & 1) * half + (row >> 5) * 17 + (row & 15)]
        product = lax.dot_general(
            picked, held[slot], (((1,), (0,)), ((), ())), preferred_element_type=jnp.float32
        )
        out[col + (col >> 5)] += jnp.where(slot < count, product * scale, 0.0)

    products(count, blocks_hbm, held, sems, prepare, step)


def kernel_call(body, outs, scratch, slots, tables, vectors, blocks):
    specs = [pl.BlockSpec(memory_space=pltpu.SMEM)] * 3
    specs += [pl.BlockSpec(memory_space=pltpu.VMEM)] * len(vectors)
    specs += [pl.BlockSpec(memory_space=pl.ANY)]
    return pl.pallas_call(
        body,
        out_shape=outs,
        in_specs=specs,
        out_specs=jax.tree.map(lambda _: pl.BlockSpec(memory_space=pltpu.VMEM), outs),
        scratch_shapes=[
            scratch,
            pltpu.VMEM((slots, LANES, LANES), jnp.bfloat16),
            pltpu.SemaphoreType.DMA((slots // CHUNK,)),
        ],
        compiler_params=pltpu.CompilerParams(vmem_limit_bytes=VMEM_BYTES),
        cost_estimate=pl.CostEstimate(
            flops=2 * slots * LANES * LANES * 16, bytes_accessed=slots * LANES * LANES * 2 + (4 << 20), transcendentals=0
        ),
    )(*tables, *vectors, blocks)


def split_squares(values):
    squares = jnp.sum(values * values, axis=(0, 2))[:, None]
    first = lax.reduce_precision(squares, 8, 7)
    second = lax.reduce_precision(squares - first, 8, 7)
    lane = lax.broadcasted_iota(jnp.int32, (squares.shape[0], LANES), 1)
    return side_lanes(lane, first, second, squares - first - second)


def spread(values, axes, copies):
    piece = jnp.concatenate([values, split_squares(values)[None]], axis=0).astype(jnp.bfloat16)
    sent = jnp.broadcast_to(piece[None], (copies,) + piece.shape)
    got = lax.all_to_all(sent, axes, 0, 0, tiled=True)
    return got.reshape((-1,) + piece.shape[1:])


def collect(sent, axes, sources, gain):
    got = lax.all_to_all(sent.astype(jnp.float16), axes, 0, 0, tiled=True)
    got = got.reshape((sources, -1) + sent.shape[1:]).astype(jnp.float32)
    exponent, squares = squares_of_side(got[:, -1])
    weight = jnp.exp2(0.5 * exponent) * (1.0 / gain)
    norm = jnp.sqrt(jnp.sum(squares, axis=0) + NORM_EPS)
    return jnp.sum(got[:, :-1] * weight[:, None, :, None], axis=0), norm


def swap_cores(values):
    return lax.ppermute(values, "c", [(0, 1), (1, 0)])


def rotation(rho_bar, phi_bar, beta_norm, alpha_norm):
    rho_new = jnp.sqrt(rho_bar * rho_bar + beta_norm * beta_norm)
    cosine = rho_bar / rho_new
    sine_val = beta_norm / rho_new
    theta_coef = sine_val * alpha_norm
    rho_next = -cosine * alpha_norm
    phi_new = cosine * phi_bar
    phi_next = sine_val * phi_bar
    return (phi_new / rho_new, theta_coef / rho_new, rho_next, phi_next)


def per_rhs(scale):
    return scale[None, :, None]


def shards(blocks, block_rows, block_cols, counts, travel_times):
    blocks_here = blocks[0, 0]
    slots = blocks_here.shape[0]
    core = lax.axis_index("c").astype(jnp.int32)
    tables = (block_rows[0, 0], block_cols[0, 0], jnp.stack([counts[0, 0], core]))
    count_rhs = travel_times.shape[0]
    block = (count_rhs, LANES)

    def rays_of(right_raw):
        right_full = spread(right_raw, DEVICES_OF_ROW, 8)
        keep, send = kernel_call(
            rays_kernel,
            [jax.ShapeDtypeStruct((8 * 17,) + block, jnp.float32)] * 2,
            pltpu.VMEM((16 * 17,) + block, jnp.float32),
            slots, tables, (right_full,), blocks_here,
        )
        both = (keep + swap_cores(send)).reshape((8, 17) + block)
        squares = both[0, 16, :, :1]
        packed, exponent = side_of_squares(squares, lax.broadcasted_iota(jnp.int32, block, 1))
        scale = RAY_GAIN * jnp.exp2(-0.5 * exponent)
        is_side = lax.broadcasted_iota(jnp.int32, (1, 17, 1, 1), 1) == 16
        sent = jnp.where(is_side, packed, both * scale)
        return collect(sent.reshape((8 * 17,) + block), CHIPS_OF_COL, 8, RAY_GAIN)

    def cells_of(left_raw):
        left_own = spread(left_raw, CHIPS_OF_COL, 8)
        left_other = swap_cores(left_own)
        out = kernel_call(
            cells_kernel,
            jax.ShapeDtypeStruct((8 * 33,) + block, jnp.float32),
            pltpu.VMEM((16 * 17,) + block, jnp.bfloat16),
            slots, tables, (left_own, left_other), blocks_here,
        )
        return collect(out, DEVICES_OF_ROW, 8, CELL_GAIN)

    def whole_norm(values):
        squares = jnp.sum(values * values, axis=(0, 2))
        sent = jnp.broadcast_to(jnp.pad(squares, (0, LANES - count_rhs)), (128, 8, LANES))
        got = lax.all_to_all(sent, ("z", "xl", "xh", "y", "c"), 0, 0, tiled=True)
        return jnp.sqrt(jnp.sum(got[:, 0, :count_rhs], axis=0) + NORM_EPS)

    left_raw = travel_times.reshape(count_rhs, -1, LANES).transpose(1, 0, 2)
    product, beta_norm = cells_of(left_raw)
    left = left_raw / per_rhs(beta_norm)
    right_raw = product / per_rhs(beta_norm)
    phi_bar = beta_norm
    solution, direction, rho_bar = None, None, None
    for iteration in range(ITERS):
        product, alpha_norm = rays_of(right_raw)
        right = right_raw / per_rhs(alpha_norm)
        if iteration == 0:
            direction, rho_bar = right, alpha_norm
        else:
            step_scale, turn_scale, rho_bar, phi_bar = rotation(rho_bar, phi_bar, beta_norm, alpha_norm)
            solution = per_rhs(step_scale) * direction
            direction = right - per_rhs(turn_scale) * direction
        left_raw = product / per_rhs(alpha_norm) - per_rhs(alpha_norm) * left
        product, beta_norm = cells_of(left_raw)
        left = left_raw / per_rhs(beta_norm)
        right_raw = product / per_rhs(beta_norm) - per_rhs(beta_norm) * right
    alpha_norm = whole_norm(right_raw)
    right = right_raw / per_rhs(alpha_norm)
    step_scale, turn_scale, rho_bar, phi_bar = rotation(rho_bar, phi_bar, beta_norm, alpha_norm)
    solution = solution + per_rhs(step_scale) * direction
    direction = right - per_rhs(turn_scale) * direction
    scaled = per_rhs(phi_bar) * direction

    def placed(values):
        return values.transpose(1, 0, 2).reshape(count_rhs, 1, 1, -1)

    return (placed(solution), placed(scaled))


def solution(mesh):
    physical = Mesh(mesh.devices.reshape(4, 2, 2, 4, 2), ("z", "xl", "xh", "y", "c"))
    row, col = ("z", "xl"), ("xh", "y", "c")
    placed = (
        P(row, col, None, None, None),
        P(row, col, None),
        P(row, col, None),
        P(row, col),
        P(None, row + col),
    )
    return jax.shard_map(
        shards,
        mesh=physical,
        in_specs=placed,
        out_specs=(P(None, col, row, None), P(None, col, row, None)),
        check_vma=False,
    )
```

time: 991 us -> 259 us (0.26)
  waiting for transfers between devices: 491 us -> 10.5 us
  blocking collectives: 391 us -> 199 us
  matrix products: 32.6 us -> 0 us
  local copies, waits for them, and re-layouts: 42.8 us -> 20.7 us
  Pallas kernels: 0 us -> 17.4 us
  between operations: 15 us -> 2 us
    psum x6 -> x0, blocking collectives: 391 us -> none  [global_norm(): lax.psum(square_sums(partial_value), ('row', 'col')) + norm_eps]
    reduce_scatter x5 -> x0, waiting for transfers between devices: 295 us -> none  [the longest x3 155 us: rows_to_cells(): lax.psum_scatter(partial_value, 'row', scatter_dimension=1, tiled=True)]
    all_to_all x0 -> x11, blocking collectives: none -> 199 us  [the longest x5 97.3 us: collect(): got = lax.all_to_all(sent.astype(jnp.float16), axes, 0, 0, tiled=True)]
    all_gather x5 -> x0, waiting for transfers between devices: 196 us -> none  [the longest x3 120 us: ray_side(): lax.all_gather((partial_value / beta_norm[:, None]).astype(jnp.bfloat16),...]
    dot_general x10 -> x0, matrix products: 32.6 us -> none  [the longest x3 11.7 us: backward_cols(): jnp.einsum('kni,nij->knj', picked, blocks_here, preferred_element_type=jn...]
    pallas_call x0 -> x5, Pallas kernels: none -> 17.4 us  [kernel_call(): pl.pallas_call(body, out_shape=outs, in_specs=specs, out_specs=jax.tree.m...]
    ppermute x0 -> x5, waiting for transfers between devices: none -> 10.5 us  [swap_cores(): return lax.ppermute(values, 'c', [(0, 1), (1, 0)])]
    unnamed x15 -> x66, local copies, waits for them, and re-layouts: 22.8 us -> 18.5 us
  transfers between devices with their start and end apart: 10 -> 5, of which waited for: 10 -> 5; matrix products, arithmetic and copies ran while one was open for 0% -> 0% of each run, Pallas kernels for 0% -> 0%
where the time goes in v1:
time: 259 us; the launch traced here: 257 us
  blocking collectives  199 us (77%)
  local copies, waits for them, and re-layouts  20.7 us (8%)
  Pallas kernels  17.4 us (7%)
  waiting for transfers between devices  10.5 us (4%)
  other arithmetic  7.08 us (3%)
    all_to_all x5, blocking collectives, collect(): got = lax.all_to_all(sent.astype(jnp.float16), axes, 0, 0, tiled=True)  97.3 us
    all_to_all x5, blocking collectives, spread(): got = lax.all_to_all(sent, axes, 0, 0, tiled=True)  84 us
    unnamed x66, local copies, waits for them, and re-layouts  18.5 us
    all_to_all x1, blocking collectives, whole_norm(): got = lax.all_to_all(sent, ('z', 'xl', 'xh', 'y', 'c'), 0, 0, tiled=True)  17.7 us
    pallas_call x5, Pallas kernels, kernel_call(): pl.pallas_call(body, out_shape=outs, in_specs=specs, out_specs=jax.tree.m...  17.4 us
    ppermute x5, waiting for transfers between devices, swap_cores(): return lax.ppermute(values, 'c', [(0, 1), (1, 0)])  10.5 us
  transfers between devices with their start and end apart: 5, of which 5 were waited for; matrix products, arithmetic and copies ran while one was open for 0% of the time, Pallas kernels for 0%

profile of v1, /device:TPU:0, one launch (start us, length us, event | category | flops | bytes accessed | tf_op | source)
XLA Modules:
  0.0 257.0 jit_solution(9765249979066998842)
XLA Ops:
  0.7 0.9 copy.78
  2.1 19.0 %all_to_all.55 = bf16[8,17,16,128]{3,2,1,0:T(8,128)(2,1)S(1)} all-to-all(bf16[8,17,16,128]{3,2,1,0:T(8,128)(2,1)S(1)} %broadcast_in_dim.227), channel_id=1, replica_groups=mesh['z'=4,'xl'=2,'xh'=2,'y'=4,'c'=2] {'xh','y'}, dimensions={0} | all-to-all | bytes 1114112 | tf_op jit(solution)/shard_map/all_to_all | solution.py:149
  21.8 1.2 collective-permute-done.left_other
  23.0 2.8 %copy-done = bf16[1,1,192,128,128]{4,3,2,1,0:T(8,128)(2,1)S(1)} copy-done((bf16[1,1,192,128,128]{4,3,2,1,0:T(8,128)(2,1)S(1)}, bf16[1,1,192,128,128]{4,3,2,1,0:T(8,128)(2,1)}, u32[]{:S(2)}) %copy-start) | copy-done | bytes 6291480
  25.8 3.1 %shard_map.68 = f32[264,16,128]{2,1,0:T(8,128)S(1)} custom-call(s32[192]{0:T(256)S(1)} %bitcast.113, s32[192]{0:T(256)S(1)} %bitcast.118, s32[2]{0:T(128)S(1)} %pad_add_fusion.scalars, bf16[136,16,128]{2,1,0:T(8,128)(2,1)S(1)} %bitcast.108, bf16[136,16,128]{2,1,0:T(8,128)(2,1)S(1)} %collective-permute-done.left_other, bf16[192,128,128]{2,1,0:T(8,128)(2,1)S(1)} %bitcast.100), custom_call_target="tpu_custom_call" | custom-call | flops 100663296 | bytes 10485760 | tf_op jit(solution)/shard_map/pallas_call | solution.py:121
  29.1 22.7 %all_to_all.56 = f16[264,16,128]{2,1,0:T(8,128)(2,1)S(1)} all-to-all(f16[264,16,128]{2,1,0:T(8,128)(2,1)S(1)} %convert_element_type.72), channel_id=1, replica_groups=mesh['z'=4,'xl'=2,'xh'=2,'y'=4,'c'=2] {'z','xl'}, dimensions={0} | all-to-all | bytes 2162688 | tf_op jit(solution)/shard_map/all_to_all | solution.py:154
  53.3 17.8 %all_to_all.57 = bf16[8,33,16,128]{3,2,1,0:T(8,128)(2,1)S(1)} all-to-all(bf16[8,33,16,128]{3,2,1,0:T(8,128)(2,1)S(1)} %broadcast_in_dim.231), channel_id=1, replica_groups=mesh['z'=4,'xl'=2,'xh'=2,'y'=4,'c'=2] {'z','xl'}, dimensions={0} | all-to-all | bytes 2162688 | tf_op jit(solution)/shard_map/all_to_all | solution.py:149
  71.1 2.8 %copy-done.1 = bf16[1,1,192,128,128]{4,3,2,1,0:T(8,128)(2,1)S(1)} copy-done((bf16[1,1,192,128,128]{4,3,2,1,0:T(8,128)(2,1)S(1)}, bf16[1,1,192,128,128]{4,3,2,1,0:T(8,128)(2,1)}, u32[]{:S(2)}) %copy-start.1) | copy-done | bytes 6291480
  73.9 4.0 %shard_map.69 = (f32[136,16,128]{2,1,0:T(8,128)S(1)}, f32[136,16,128]{2,1,0:T(8,128)S(1)}) custom-call(s32[192]{0:T(256)S(1)} %bitcast.114, s32[192]{0:T(256)S(1)} %bitcast.119, s32[2]{0:T(128)S(1)} %pad_add_fusion.scalars, bf16[264,16,128]{2,1,0:T(8,128)(2,1)S(1)} %bitcast.105, bf16[192,128,128]{2,1,0:T(8,128)(2,1)S(1)} %bitcast.101), custom_call_target="tpu_custom_call" | custom-call | flops 100663296 | bytes 10485760 | tf_op jit(solution)/shard_map/pallas_call | solution.py:121
  78.1 2.8 %collective-permute-done.1 = f32[136,16,128]{2,1,0:T(8,128)} collective-permute-done((f32[136,16,128]{2,1,0:T(8,128)S(1)}, f32[136,16,128]{2,1,0:T(8,128)}, u32[]{:S(2)}, u32[]{:S(2)}) %collective-permute-start.1) | collective-permute-done | bytes 1114144 | tf_op jit(solution)/shard_map/ppermute | solution.py:163
  80.9 1.4 add.174
  82.9 17.4 %all_to_all.58 = f16[136,16,128]{2,1,0:T(8,128)(2,1)S(1)} all-to-all(f16[136,16,128]{2,1,0:T(8,128)(2,1)S(1)} %select_convert_fusion.1), channel_id=1, replica_groups=mesh['z'=4,'xl'=2,'xh'=2,'y'=4,'c'=2] {'xh','y'}, dimensions={0} | all-to-all | bytes 1114112 | tf_op jit(solution)/shard_map/all_to_all | solution.py:154
  101.7 0.4 copy-done.7
  102.2 14.2 %all_to_all.59 = bf16[8,17,16,128]{3,2,1,0:T(8,128)(2,1)S(1)} all-to-all(bf16[8,17,16,128]{3,2,1,0:T(8,128)(2,1)S(1)} %broadcast_in_dim.240), channel_id=1, replica_groups=mesh['z'=4,'xl'=2,'xh'=2,'y'=4,'c'=2] {'xh','y'}, dimensions={0} | all-to-all | bytes 1114112 | tf_op jit(solution)/shard_map/all_to_all | solution.py:149
  116.4 2.0 collective-permute-done.2.left_other
  118.4 2.8 %copy-done.2 = bf16[1,1,192,128,128]{4,3,2,1,0:T(8,128)(2,1)S(1)} copy-done((bf16[1,1,192,128,128]{4,3,2,1,0:T(8,128)(2,1)S(1)}, bf16[1,1,192,128,128]{4,3,2,1,0:T(8,128)(2,1)}, u32[]{:S(2)}) %copy-start.2) | copy-done | bytes 6291480
  121.2 3.1 %shard_map.70 = f32[264,16,128]{2,1,0:T(8,128)S(1)} custom-call(s32[192]{0:T(256)S(1)} %bitcast.115, s32[192]{0:T(256)S(1)} %bitcast.120, s32[2]{0:T(128)S(1)} %pad_add_fusion.scalars, bf16[136,16,128]{2,1,0:T(8,128)(2,1)S(1)} %bitcast.112, bf16[136,16,128]{2,1,0:T(8,128)(2,1)S(1)} %collective-permute-done.2.left_other, bf16[192,128,128]{2,1,0:T(8,128)(2,1)S(1)} %bitcast.102), custom_call_target="tpu_custom_call" | custom-call | flops 100663296 | bytes 10485760 | tf_op jit(solution)/shard_map/pallas_call | solution.py:121
  124.5 20.4 %all_to_all.60 = f16[264,16,128]{2,1,0:T(8,128)(2,1)S(1)} all-to-all(f16[264,16,128]{2,1,0:T(8,128)(2,1)S(1)} %convert_element_type.78), channel_id=1, replica_groups=mesh['z'=4,'xl'=2,'xh'=2,'y'=4,'c'=2] {'z','xl'}, dimensions={0} | all-to-all | bytes 2162688 | tf_op jit(solution)/shard_map/all_to_all | solution.py:154
  146.5 18.7 %all_to_all.61 = bf16[8,33,16,128]{3,2,1,0:T(8,128)(2,1)S(1)} all-to-all(bf16[8,33,16,128]{3,2,1,0:T(8,128)(2,1)S(1)} %broadcast_in_dim.244), channel_id=1, replica_groups=mesh['z'=4,'xl'=2,'xh'=2,'y'=4,'c'=2] {'z','xl'}, dimensions={0} | all-to-all | bytes 2162688 | tf_op jit(solution)/shard_map/all_to_all | solution.py:149
  165.2 2.8 %copy-done.3 = bf16[1,1,192,128,128]{4,3,2,1,0:T(8,128)(2,1)S(1)} copy-done((bf16[1,1,192,128,128]{4,3,2,1,0:T(8,128)(2,1)S(1)}, bf16[1,1,192,128,128]{4,3,2,1,0:T(8,128)(2,1)}, u32[]{:S(2)}) %copy-start.3) | copy-done | bytes 6291480
  168.0 4.0 %shard_map.71 = (f32[136,16,128]{2,1,0:T(8,128)S(1)}, f32[136,16,128]{2,1,0:T(8,128)S(1)}) custom-call(s32[192]{0:T(256)S(1)} %bitcast.116, s32[192]{0:T(256)S(1)} %bitcast.121, s32[2]{0:T(128)S(1)} %pad_add_fusion.scalars, bf16[264,16,128]{2,1,0:T(8,128)(2,1)S(1)} %bitcast.106, bf16[192,128,128]{2,1,0:T(8,128)(2,1)S(1)} %bitcast.103), custom_call_target="tpu_custom_call" | custom-call | flops 100663296 | bytes 10485760 | tf_op jit(solution)/shard_map/pallas_call | solution.py:121
  172.3 2.6 %collective-permute-done.3 = f32[136,16,128]{2,1,0:T(8,128)S(1)} collective-permute-done((f32[136,16,128]{2,1,0:T(8,128)S(1)}, f32[136,16,128]{2,1,0:T(8,128)S(1)}, u32[]{:S(2)}, u32[]{:S(2)}) %collective-permute-start.3) | collective-permute-done | bytes 1114144 | tf_op jit(solution)/shard_map/ppermute | solution.py:163
  175.9 16.1 %all_to_all.62 = f16[136,16,128]{2,1,0:T(8,128)(2,1)S(1)} all-to-all(f16[136,16,128]{2,1,0:T(8,128)(2,1)S(1)} %select_convert_fusion), channel_id=1, replica_groups=mesh['z'=4,'xl'=2,'xh'=2,'y'=4,'c'=2] {'xh','y'}, dimensions={0} | all-to-all | bytes 1114112 | tf_op jit(solution)/shard_map/all_to_all | solution.py:154
  192.5 0.5 copy-done.8
  193.3 14.2 %all_to_all.63 = bf16[8,17,16,128]{3,2,1,0:T(8,128)(2,1)S(1)} all-to-all(bf16[8,17,16,128]{3,2,1,0:T(8,128)(2,1)S(1)} %broadcast_in_dim.252), channel_id=1, replica_groups=mesh['z'=4,'xl'=2,'xh'=2,'y'=4,'c'=2] {'xh','y'}, dimensions={0} | all-to-all | bytes 1114112 | tf_op jit(solution)/shard_map/all_to_all | solution.py:149
  207.6 2.0 collective-permute-done.4.left_other
  209.5 2.8 %copy-done.4 = bf16[1,1,192,128,128]{4,3,2,1,0:T(8,128)(2,1)S(1)} copy-done((bf16[1,1,192,128,128]{4,3,2,1,0:T(8,128)(2,1)S(1)}, bf16[1,1,192,128,128]{4,3,2,1,0:T(8,128)(2,1)}, u32[]{:S(2)}) %copy-start.4) | copy-done | bytes 6291480
  212.3 3.1 %shard_map.72 = f32[264,16,128]{2,1,0:T(8,128)S(1)} custom-call(s32[192]{0:T(256)S(1)} %bitcast.117, s32[192]{0:T(256)S(1)} %bitcast.122, s32[2]{0:T(128)S(1)} %pad_add_fusion.scalars, bf16[136,16,128]{2,1,0:T(8,128)(2,1)S(1)} %bitcast.110, bf16[136,16,128]{2,1,0:T(8,128)(2,1)S(1)} %collective-permute-done.4.left_other, bf16[192,128,128]{2,1,0:T(8,128)(2,1)S(1)} %bitcast.104), custom_call_target="tpu_custom_call" | custom-call | flops 100663296 | bytes 10485760 | tf_op jit(solution)/shard_map/pallas_call | solution.py:121
  215.6 20.6 %all_to_all.64 = f16[264,16,128]{2,1,0:T(8,128)(2,1)S(1)} all-to-all(f16[264,16,128]{2,1,0:T(8,128)(2,1)S(1)} %convert_element_type.84), channel_id=1, replica_groups=mesh['z'=4,'xl'=2,'xh'=2,'y'=4,'c'=2] {'z','xl'}, dimensions={0} | all-to-all | bytes 2162688 | tf_op jit(solution)/shard_map/all_to_all | solution.py:154
  237.2 17.7 %all_to_all.65 = f32[128,8,128]{2,1,0:T(8,128)S(1)} all-to-all(f32[128,8,128]{2,1,0:T(8,128)S(1)} %broadcast_in_dim.253), channel_id=1, replica_groups=mesh['z'=4,'xl'=2,'xh'=2,'y'=4,'c'=2] {'z','xl','xh','y','c'}, dimensions={0} | all-to-all | bytes 1048576 | tf_op jit(solution)/shard_map/all_to_all | solution.py:219
  255.4 0.8 copy.66
  256.2 0.8 copy.64
  (149 shorter events, 9.5 us)
Async XLA Ops:
  0.7 20.4 %copy-start.10 = (pred[128]{0:T(512)(128)(4,1)}, pred[128]{0:T(512)(128)(4,1)S(1)}, u32[]{:S(2)}) copy-start(pred[128]{0:T(512)(128)(4,1)S(1)} %get-tuple-element.68) | copy-start | bytes 388
  0.7 20.4 %copy-start.14 = (pred[128]{0:T(512)(128)(4,1)}, pred[128]{0:T(512)(128)(4,1)S(1)}, u32[]{:S(2)}) copy-start(pred[128]{0:T(512)(128)(4,1)S(1)} %get-tuple-element.69) | copy-start | bytes 388
  1.8 21.2 %copy-start.5 = (s32[1,1,192]{2,1,0:T(1,128)S(1)}, s32[1,1,192]{2,1,0:T(1,128)}, u32[]{:S(2)}) copy-start(s32[1,1,192]{2,1,0:T(1,128)} %param.6) | copy-start | bytes 2308
  1.8 21.2 %copy-start.6 = (s32[1,1,192]{2,1,0:T(1,128)S(1)}, s32[1,1,192]{2,1,0:T(1,128)}, u32[]{:S(2)}) copy-start(s32[1,1,192]{2,1,0:T(1,128)} %param.7) | copy-start | bytes 2308
  21.1 2.0 collective-permute-start
  23.0 2.8 %copy-start = (bf16[1,1,192,128,128]{4,3,2,1,0:T(8,128)(2,1)S(1)}, bf16[1,1,192,128,128]{4,3,2,1,0:T(8,128)(2,1)}, u32[]{:S(2)}) copy-start(bf16[1,1,192,128,128]{4,3,2,1,0:T(8,128)(2,1)} %param.5) | copy-start | bytes 18874372
  52.3 0.8 copy-start.11
  52.3 0.8 copy-start.15
  71.1 2.8 %copy-start.1 = (bf16[1,1,192,128,128]{4,3,2,1,0:T(8,128)(2,1)S(1)}, bf16[1,1,192,128,128]{4,3,2,1,0:T(8,128)(2,1)}, u32[]{:S(2)}) copy-start(bf16[1,1,192,128,128]{4,3,2,1,0:T(8,128)(2,1)} %param.5) | copy-start | bytes 18874372
  77.9 3.0 %collective-permute-start.1 = (f32[136,16,128]{2,1,0:T(8,128)S(1)}, f32[136,16,128]{2,1,0:T(8,128)}, u32[]{:S(2)}, u32[]{:S(2)}) collective-permute-start(f32[136,16,128]{2,1,0:T(8,128)S(1)} %get-tuple-element.7), channel_id=1, source_target_pairs={{0,1},{1,0},{2,3},{3,2},{4,5},{5,4},{6,7},{7,6},{8,9},{9,8},{10,11... | collective-permute-start | bytes 3342344 | tf_op jit(solution)/shard_map/ppermute | solution.py:163
  78.1 4.4 %copy-start.27 = (pred[136]{0:T(512)(128)(4,1)}, pred[136]{0:T(512)(128)(4,1)S(1)}, u32[]{:S(2)}) copy-start(pred[136]{0:T(512)(128)(4,1)S(1)} %broadcast_in_dim.221) | copy-start | bytes 412
  80.9 1.5 copy-start.12
  80.9 1.6 copy-start.16
  100.4 0.7 copy-start.19
  100.4 0.9 copy-start.9
  100.7 1.5 copy-start.21
  101.1 44.8 %copy-start.23 = (f32[16]{0:T(128)}, f32[16]{0:T(128)S(1)}, u32[]{:S(2)}) copy-start(f32[16]{0:T(128)S(1)} %get-tuple-element.56) | copy-start | bytes 196
  101.4 0.7 copy-start.7
  116.4 2.0 collective-permute-start.2
  118.4 2.8 %copy-start.2 = (bf16[1,1,192,128,128]{4,3,2,1,0:T(8,128)(2,1)S(1)}, bf16[1,1,192,128,128]{4,3,2,1,0:T(8,128)(2,1)}, u32[]{:S(2)}) copy-start(bf16[1,1,192,128,128]{4,3,2,1,0:T(8,128)(2,1)} %param.5) | copy-start | bytes 18874372
  145.6 0.6 copy-start.13
  145.6 0.7 copy-start.17
  165.2 2.8 %copy-start.3 = (bf16[1,1,192,128,128]{4,3,2,1,0:T(8,128)(2,1)S(1)}, bf16[1,1,192,128,128]{4,3,2,1,0:T(8,128)(2,1)}, u32[]{:S(2)}) copy-start(bf16[1,1,192,128,128]{4,3,2,1,0:T(8,128)(2,1)} %param.5) | copy-start | bytes 18874372
  172.1 2.8 %collective-permute-start.3 = (f32[136,16,128]{2,1,0:T(8,128)S(1)}, f32[136,16,128]{2,1,0:T(8,128)S(1)}, u32[]{:S(2)}, u32[]{:S(2)}) collective-permute-start(f32[136,16,128]{2,1,0:T(8,128)S(1)} %get-tuple-element.9), channel_id=1, source_target_pairs={{0,1},{1,0},{2,3},{3,2},{4,5},{5,4},{6,7},{7,6},{8,9},{9,8},{10,11... | collective-permute-start | bytes 3342344 | tf_op jit(solution)/shard_map/ppermute | solution.py:163
  174.9 0.6 copy-start.28
  192.0 0.9 copy-start.8
  207.6 2.0 collective-permute-start.4
  209.5 2.8 %copy-start.4 = (bf16[1,1,192,128,128]{4,3,2,1,0:T(8,128)(2,1)S(1)}, bf16[1,1,192,128,128]{4,3,2,1,0:T(8,128)(2,1)}, u32[]{:S(2)}) copy-start(bf16[1,1,192,128,128]{4,3,2,1,0:T(8,128)(2,1)} %param.5) | copy-start | bytes 18874372
  236.9 18.2 %copy-start.22 = (f32[16]{0:T(128)S(1)}, f32[16]{0:T(128)}, u32[]{:S(2)}) copy-start(f32[16]{0:T(128)} %copy-done.21) | copy-start | bytes 196
  236.9 18.2 %copy-start.26 = (f32[16]{0:T(128)S(1)}, f32[16]{0:T(128)}, u32[]{:S(2)}) copy-start(f32[16]{0:T(128)} %copy-done.25) | copy-start | bytes 196
  236.9 18.2 %copy-start.20 = (f32[16]{0:T(128)S(1)}, f32[16]{0:T(128)}, u32[]{:S(2)}) copy-start(f32[16]{0:T(128)} %copy-done.18) | copy-start | bytes 196
  236.9 18.3 %copy-start.24 = (f32[16]{0:T(128)S(1)}, f32[16]{0:T(128)}, u32[]{:S(2)}) copy-start(f32[16]{0:T(128)} %copy-done.23) | copy-start | bytes 196
  (2 other events, 1.1 us)

commit v2 on v1

v2 whole, which is shorter than its diff:
```python
import functools

import jax
import jax.numpy as jnp
from jax import lax
from jax.experimental import pallas as pl
from jax.experimental.pallas import tpu as pltpu
from jax.sharding import Mesh, PartitionSpec as P

LANES = 128
NORM_EPS = 1e-06
SQUARES_FLOOR = 1e-30
CELL_GAIN = 4096.0
RAY_GAIN = 2048.0
CHUNK = 64
CHIPS_OF_COL = ("xh", "y")
DEVICES_OF_ROW = ("z", "xl")
VMEM_BYTES = 32 << 20


def exponent_of(squares):
    return jnp.ceil(jnp.log2(jnp.maximum(squares, SQUARES_FLOOR)))


def side_lanes(lane, first, second, third):
    return jnp.where(lane == 0, first, jnp.where(lane == 1, second, jnp.where(lane == 2, third, 0.0)))


def side_of_squares(squares, lane):
    exponent = exponent_of(squares)
    fraction = squares * jnp.exp2(-exponent)
    upper = jnp.floor(fraction * 1024.0)
    return side_lanes(lane, exponent, upper, fraction * 1024.0 - upper), exponent


def pair_products(count, vector, held, source, visit):
    def chunk(at, carry):
        for step in range(0, CHUNK, 2):
            slot = at * CHUNK + step
            picked = jnp.concatenate([vector[source(slot)], vector[source(slot + 1)]], axis=0)
            pair = jnp.concatenate([held[slot], held[slot + 1]], axis=1)
            both = lax.dot_general(picked, pair, (((1,), (0,)), ((), ())), preferred_element_type=jnp.float32)
            rhs = both.shape[0] // 2
            visit(slot, both[:rhs, :LANES])
            visit(slot + 1, both[rhs:, LANES:])
        return carry

    lax.fori_loop(0, (count + (CHUNK - 1)) // CHUNK, chunk, 0)


def rays_kernel(rows, cols, scalars, right, turned, keep, send, total):
    count, core = scalars[0], scalars[1]
    half = keep.shape[0]
    total[...] = jnp.zeros_like(total)
    side = sum(right[33 * at + 32].astype(jnp.float32) for at in range(8))
    squares = jnp.broadcast_to(jnp.sum(side, axis=1, keepdims=True), side.shape)

    def source(slot):
        col = cols[slot]
        return col + (col >> 5)

    def visit(slot, product):
        row = rows[slot]
        place = (((row >> 4) & 1) ^ core) * half + (row >> 5) * 17 + (row & 15)
        place = jnp.where(slot < count, place, 16)
        total[place] += product

    pair_products(count, right, turned, source, visit)
    for at in range(16):
        total[17 * at + 16] = squares
    keep[...] = total[:half]
    send[...] = total[half:]


def cells_kernel(turn, rows, cols, scalars, left_own, left_other, held, out, *rest):
    left = rest[-1]
    count, core = scalars[0], scalars[1]
    half = left_own.shape[0]
    left[pl.ds(core * half, half)] = left_own[...]
    left[pl.ds((1 - core) * half, half)] = left_other[...]
    out[...] = jnp.zeros_like(out)
    side = sum(left[17 * at + 16].astype(jnp.float32) for at in range(16))
    squares = jnp.broadcast_to(jnp.sum(side, axis=1, keepdims=True), side.shape)
    lane = lax.broadcasted_iota(jnp.int32, side.shape, 1)
    packed, exponent = side_of_squares(squares, lane)
    scale = CELL_GAIN * jnp.exp2(-0.5 * exponent)

    def source(slot):
        row = rows[slot]
        return ((row >> 4) & 1) * half + (row >> 5) * 17 + (row & 15)

    def visit(slot, product):
        col = cols[slot]
        place = jnp.where(slot < count, col + (col >> 5), 32)
        out[place] += product * scale
        if turn:
            rest[0][slot] = held[slot].T

    pair_products(count, left, held, source, visit)
    for at in range(8):
        out[33 * at + 32] = packed


def send_blocks(sent, values, squares):
    size = sent.shape[0] // 8
    for at, value in enumerate(values):
        rounded = value.astype(jnp.bfloat16)
        for copy in range(8):
            sent[size * copy + at] = rounded
    squares = jnp.sum(squares, axis=1, keepdims=True)
    first = squares.astype(jnp.bfloat16).astype(jnp.float32)
    second = (squares - first).astype(jnp.bfloat16).astype(jnp.float32)
    lane = lax.broadcasted_iota(jnp.int32, (squares.shape[0], LANES), 1)
    side = side_lanes(lane, first, second, squares - first - second).astype(jnp.bfloat16)
    for copy in range(8):
        sent[size * copy + size - 1] = side


def start_kernel(times, sent, raw):
    squares = jnp.zeros(raw.shape[1:], jnp.float32)
    for at in range(raw.shape[0]):
        value = times[:, LANES * at : LANES * (at + 1)]
        raw[at] = value
        squares += value * value
    send_blocks(sent, [times[:, LANES * at : LANES * (at + 1)] for at in range(raw.shape[0])], squares)


def core_kernel(keep, received, out):
    squares = keep[16] + received[16]
    lane = lax.broadcasted_iota(jnp.int32, squares.shape, 1)
    packed, exponent = side_of_squares(squares, lane)
    scale = RAY_GAIN * jnp.exp2(-0.5 * exponent)
    for chip in range(8):
        for at in range(16):
            out[17 * chip + at] = (keep[17 * chip + at] + received[17 * chip + at]) * scale
        out[17 * chip + 16] = packed


def update_kernel(gain, first, last, got, *rest):
    previous, (raw, norm_out, tail) = rest[:-3], rest[-3:]
    size = raw.shape[0] + 1
    weights, total = [], 0.0
    for source in range(8):
        side = got[size * source + size - 1]
        exponent = side[:, 0:1]
        weights.append(jnp.broadcast_to(jnp.exp2(0.5 * exponent) * (1.0 / gain), side.shape))
        total += (side[:, 1:2] + side[:, 2:3]) * (1.0 / 1024.0) * jnp.exp2(exponent)
    norm = jnp.sqrt(jnp.broadcast_to(total, raw.shape[1:]) + NORM_EPS)
    norm_out[...] = norm
    inverse = 1.0 / norm
    weights = [weight * inverse for weight in weights]
    if not first:
        past = norm / previous[1][...]
    squares = jnp.zeros(raw.shape[1:], jnp.float32)
    values = []
    for at in range(size - 1):
        value = got[at] * weights[0]
        for source in range(1, 8):
            value += got[size * source + at] * weights[source]
        if not first:
            value -= previous[0][at] * past
        raw[at] = value
        squares += value * value
        values.append(value)
    if last:
        squares = jnp.broadcast_to(jnp.sum(squares, axis=1, keepdims=True), squares.shape)
        tail[...] = jnp.sum(jnp.where(diagonal(squares.shape), squares, 0.0), axis=0, keepdims=True)
    else:
        send_blocks(tail, [raw[at] for at in range(size - 1)], squares)


def diagonal(shape):
    return lax.broadcasted_iota(jnp.int32, shape, 0) == lax.broadcasted_iota(jnp.int32, shape, 1)


def finish_kernel(sums, raw0, raw1, raw2, alpha0, alpha1, beta0, beta1, beta2, solution_out, scaled_out):
    shape = alpha0.shape
    total = jnp.broadcast_to(jnp.sum(sums[:, 0, :], axis=0, keepdims=True), shape)
    total = jnp.sum(jnp.where(diagonal(shape), total, 0.0), axis=1, keepdims=True)
    alpha2 = jnp.sqrt(jnp.broadcast_to(total, shape) + NORM_EPS)
    phi_bar, rho_bar = beta0[...], alpha0[...]
    step1, turn1, rho_bar, phi_bar = rotation(rho_bar, phi_bar, beta1[...], alpha1[...])
    step2, turn2, rho_bar, phi_bar = rotation(rho_bar, phi_bar, beta2[...], alpha2)
    over0, over1, over2 = 1.0 / alpha0[...], 1.0 / alpha1[...], 1.0 / alpha2
    for at in range(raw0.shape[0]):
        lanes = slice(LANES * at, LANES * (at + 1))
        direction0 = raw0[at] * over0
        direction1 = raw1[at] * over1 - turn1 * direction0
        direction2 = raw2[at] * over2 - turn2 * direction1
        solution_out[:, lanes] = step1 * direction0 + step2 * direction1
        scaled_out[:, lanes] = phi_bar * direction2


def small_call(body, outs, *args):
    return pl.pallas_call(
        body,
        out_shape=outs,
        in_specs=[pl.BlockSpec(memory_space=pltpu.VMEM)] * len(args),
        out_specs=[pl.BlockSpec(memory_space=pltpu.VMEM)] * len(outs),
        compiler_params=pltpu.CompilerParams(vmem_limit_bytes=VMEM_BYTES),
    )(*args)


def kernel_call(body, outs, scratch, tables, vectors, blocks):
    specs = [pl.BlockSpec(memory_space=pltpu.SMEM)] * 3
    specs += [pl.BlockSpec(memory_space=pltpu.VMEM)] * (len(vectors) + 1)
    slots = blocks.shape[0]
    return pl.pallas_call(
        body,
        out_shape=outs,
        in_specs=specs,
        out_specs=[pl.BlockSpec(memory_space=pltpu.VMEM)] * len(outs),
        scratch_shapes=[scratch],
        compiler_params=pltpu.CompilerParams(vmem_limit_bytes=VMEM_BYTES),
        cost_estimate=pl.CostEstimate(
            flops=2 * slots * LANES * LANES * 16, bytes_accessed=slots * LANES * LANES * 2 + (4 << 20), transcendentals=0
        ),
    )(*tables, *vectors, blocks)


def exchange(sent, axes):
    return lax.all_to_all(sent, axes, 0, 0, tiled=True)


def exchange_halves(sent, axes):
    return exchange(sent.astype(jnp.float16), axes).astype(jnp.float32)


def swap_cores(values):
    return lax.ppermute(values, "c", [(0, 1), (1, 0)])


def rotation(rho_bar, phi_bar, beta_norm, alpha_norm):
    rho_new = jnp.sqrt(rho_bar * rho_bar + beta_norm * beta_norm)
    cosine = rho_bar / rho_new
    sine_val = beta_norm / rho_new
    theta_coef = sine_val * alpha_norm
    rho_next = -cosine * alpha_norm
    phi_new = cosine * phi_bar
    phi_next = sine_val * phi_bar
    return (phi_new / rho_new, theta_coef / rho_new, rho_next, phi_next)


def shards(blocks, block_rows, block_cols, counts, travel_times):
    blocks_here = blocks[0, 0]
    core = lax.axis_index("c").astype(jnp.int32)
    tables = (block_rows[0, 0], block_cols[0, 0], jnp.stack([counts[0, 0], core]))
    count_rhs = travel_times.shape[0]
    block = (count_rhs, LANES)
    shape = jax.ShapeDtypeStruct
    rays_sent = shape((8 * 17,) + block, jnp.bfloat16)
    cells_sent = shape((8 * 33,) + block, jnp.bfloat16)
    one = shape(block, jnp.float32)

    def rays_of(sent, turned, left_raw, beta):
        right_full = exchange(sent, DEVICES_OF_ROW)
        keep, send = kernel_call(
            rays_kernel,
            [shape((8 * 17,) + block, jnp.float32)] * 2,
            pltpu.VMEM((16 * 17,) + block, jnp.float32),
            tables, (right_full,), turned,
        )
        (both,) = small_call(core_kernel, [shape((8 * 17,) + block, jnp.float32)], keep, swap_cores(send))
        got = exchange_halves(both, CHIPS_OF_COL)
        outs = [shape((16,) + block, jnp.float32), one, rays_sent]
        return small_call(functools.partial(update_kernel, RAY_GAIN, False, False), outs, got, left_raw, beta)

    def cells_of(sent, *previous, last=False):
        first = not previous
        left_own = exchange(sent, CHIPS_OF_COL)
        outs = [shape((8 * 33,) + block, jnp.float32)]
        if first:
            outs.append(shape(blocks_here.shape, blocks_here.dtype))
        out, *turned = kernel_call(
            functools.partial(cells_kernel, first),
            outs,
            pltpu.VMEM((16 * 17,) + block, jnp.bfloat16),
            tables, (left_own, swap_cores(left_own)), blocks_here,
        )
        got = exchange_halves(out, DEVICES_OF_ROW)
        outs = [shape((32,) + block, jnp.float32), one, shape((1, LANES), jnp.float32) if last else cells_sent]
        return (*small_call(functools.partial(update_kernel, CELL_GAIN, first, last), outs, got, *previous), *turned)

    sent, left_raw = small_call(start_kernel, [rays_sent, shape((16,) + block, jnp.float32)], travel_times)
    raw0, beta0, sent, turned = cells_of(sent)
    left_raw, alpha0, sent = rays_of(sent, turned, left_raw, beta0)
    raw1, beta1, sent = cells_of(sent, raw0, alpha0)
    left_raw, alpha1, sent = rays_of(sent, turned, left_raw, beta1)
    raw2, beta2, squares = cells_of(sent, raw1, alpha1, last=True)
    squares = squares + swap_cores(squares)
    sums = exchange(jnp.broadcast_to(squares, (64, 1, LANES)), DEVICES_OF_ROW + CHIPS_OF_COL)
    flat = shape((count_rhs, 32 * LANES), jnp.float32)
    outs = small_call(finish_kernel, [flat] * 2, sums, raw0, raw1, raw2, alpha0, alpha1, beta0, beta1, beta2)
    return tuple(out.reshape(count_rhs, 1, 1, -1) for out in outs)


def solution(mesh):
    physical = Mesh(mesh.devices.reshape(4, 2, 2, 4, 2), ("z", "xl", "xh", "y", "c"))
    row, col = ("z", "xl"), ("xh", "y", "c")
    placed = (
        P(row, col, None, None, None),
        P(row, col, None),
        P(row, col, None),
        P(row, col),
        P(None, row + col),
    )
    return jax.shard_map(
        shards,
        mesh=physical,
        in_specs=placed,
        out_specs=(P(None, col, row, None), P(None, col, row, None)),
        check_vma=False,
    )
```

time: 259 us -> 225 us (0.87)
  local copies, waits for them, and re-layouts: 20.7 us -> 5.66 us
  blocking collectives: 199 us -> 191 us
  other arithmetic: 7.08 us -> 1.32 us
  Pallas kernels: 17.4 us -> 12.7 us
    unnamed x66 -> x14, local copies, waits for them, and re-layouts: 18.5 us -> 5.64 us
    all_to_all x11, blocking collectives: 199 us -> 191 us  [exchange(): return lax.all_to_all(sent, axes, 0, 0, tiled=True)]
    pallas_call x5 -> x14, Pallas kernels: 17.4 us -> 12.7 us  [the longest x5 9.53 us: kernel_call(): pl.pallas_call(body, out_shape=outs, in_specs=specs, out_specs=[pl.BlockS...]
    ppermute x5 -> x6, waiting for transfers between devices: 10.5 us -> 11.8 us  [swap_cores(): return lax.ppermute(values, 'c', [(0, 1), (1, 0)])]
  transfers between devices with their start and end apart: 5 -> 6, of which waited for: 5 -> 6; matrix products, arithmetic and copies ran while one was open for 0% -> 0% of each run, Pallas kernels for 0% -> 0%
where the time goes in v2:
time: 225 us
  blocking collectives  191 us (85%)
  Pallas kernels  12.7 us (6%)
  waiting for transfers between devices  11.8 us (5%)
  local copies, waits for them, and re-layouts  5.66 us (3%)
    all_to_all x11, blocking collectives, exchange(): return lax.all_to_all(sent, axes, 0, 0, tiled=True)  191 us
    ppermute x6, waiting for transfers between devices, swap_cores(): return lax.ppermute(values, 'c', [(0, 1), (1, 0)])  11.8 us
    pallas_call x5, Pallas kernels, kernel_call(): pl.pallas_call(body, out_shape=outs, in_specs=specs, out_specs=[pl.BlockS...  9.53 us
    unnamed x14, local copies, waits for them, and re-layouts  5.64 us
  transfers between devices with their start and end apart: 6, of which 6 were waited for; matrix products, arithmetic and copies ran while one was open for 0% of the time, Pallas kernels for 0%

profile of v2, /device:TPU:0, one launch (start us, length us, event | category | flops | bytes accessed | tf_op | source)
XLA Modules:
  0.0 224.5 jit_solution(10015539864911929189)
XLA Ops:
  0.6 0.9 copy-done.1
  1.6 19.0 %all_to_all.55.left_own = bf16[136,16,128]{2,1,0:T(8,128)(2,1)S(1)} all-to-all(bf16[136,16,128]{2,1,0:T(8,128)(2,1)S(1)} %get-tuple-element.26), channel_id=1, replica_groups=mesh['z'=4,'xl'=2,'xh'=2,'y'=4,'c'=2] {'xh','y'}, dimensions={0} | all-to-all | bytes 1114112 | tf_op jit(solution)/shard_map/all_to_all | solution.py:222
  21.3 1.2 collective-permute-done.left_other
  22.6 2.8 %copy-done = bf16[1,1,192,128,128]{4,3,2,1,0:T(8,128)(2,1)S(1)} copy-done((bf16[1,1,192,128,128]{4,3,2,1,0:T(8,128)(2,1)S(1)}, bf16[1,1,192,128,128]{4,3,2,1,0:T(8,128)(2,1)}, u32[]{:S(2)}) %copy-start) | copy-done | bytes 6291480
  25.4 2.1 shard_map.69
  27.7 22.4 %all_to_all.56 = f16[264,16,128]{2,1,0:T(8,128)(2,1)S(1)} all-to-all(f16[264,16,128]{2,1,0:T(8,128)(2,1)S(1)} %convert_element_type.30), channel_id=1, replica_groups=mesh['z'=4,'xl'=2,'xh'=2,'y'=4,'c'=2] {'z','xl'}, dimensions={0} | all-to-all | bytes 2162688 | tf_op jit(solution)/shard_map/all_to_all | solution.py:222
  50.1 0.2 convert_element_type.31.got
  50.3 0.4 shard_map.70
  50.7 18.4 %all_to_all.57.right = bf16[264,16,128]{2,1,0:T(8,128)(2,1)S(1)} all-to-all(bf16[264,16,128]{2,1,0:T(8,128)(2,1)S(1)} %get-tuple-element.28), channel_id=1, replica_groups=mesh['z'=4,'xl'=2,'xh'=2,'y'=4,'c'=2] {'z','xl'}, dimensions={0} | all-to-all | bytes 2162688 | tf_op jit(solution)/shard_map/all_to_all | solution.py:222
  69.1 1.9 shard_map.71
  71.1 2.7 %collective-permute-done.1.received = f32[136,16,128]{2,1,0:T(8,128)S(1)} collective-permute-done((f32[136,16,128]{2,1,0:T(8,128)S(1)}, f32[136,16,128]{2,1,0:T(8,128)S(1)}, u32[]{:S(2)}, u32[]{:S(2)}) %collective-permute-start.1) | collective-permute-done | bytes 1114144 | tf_op jit(solution)/shard_map/ppermute | solution.py:230
  74.0 15.3 %all_to_all.58 = f16[136,16,128]{2,1,0:T(8,128)(2,1)S(1)} all-to-all(f16[136,16,128]{2,1,0:T(8,128)(2,1)S(1)} %convert_element_type.32), channel_id=1, replica_groups=mesh['z'=4,'xl'=2,'xh'=2,'y'=4,'c'=2] {'xh','y'}, dimensions={0} | all-to-all | bytes 1114112 | tf_op jit(solution)/shard_map/all_to_all | solution.py:222
  89.4 0.3 shard_map.73
  89.7 14.2 %all_to_all.59.left_own = bf16[136,16,128]{2,1,0:T(8,128)(2,1)S(1)} all-to-all(bf16[136,16,128]{2,1,0:T(8,128)(2,1)S(1)} %get-tuple-element.34), channel_id=1, replica_groups=mesh['z'=4,'xl'=2,'xh'=2,'y'=4,'c'=2] {'xh','y'}, dimensions={0} | all-to-all | bytes 1114112 | tf_op jit(solution)/shard_map/all_to_all | solution.py:222
  104.0 2.0 collective-permute-done.2.left_other
  106.0 1.8 shard_map.74
  107.9 20.2 %all_to_all.60 = f16[264,16,128]{2,1,0:T(8,128)(2,1)S(1)} all-to-all(f16[264,16,128]{2,1,0:T(8,128)(2,1)S(1)} %convert_element_type.34), channel_id=1, replica_groups=mesh['z'=4,'xl'=2,'xh'=2,'y'=4,'c'=2] {'z','xl'}, dimensions={0} | all-to-all | bytes 2162688 | tf_op jit(solution)/shard_map/all_to_all | solution.py:222
  128.3 0.5 shard_map.75
  128.7 18.3 %all_to_all.61.right = bf16[264,16,128]{2,1,0:T(8,128)(2,1)S(1)} all-to-all(bf16[264,16,128]{2,1,0:T(8,128)(2,1)S(1)} %get-tuple-element.37), channel_id=1, replica_groups=mesh['z'=4,'xl'=2,'xh'=2,'y'=4,'c'=2] {'z','xl'}, dimensions={0} | all-to-all | bytes 2162688 | tf_op jit(solution)/shard_map/all_to_all | solution.py:222
  147.1 1.9 shard_map.76
  149.1 2.7 %collective-permute-done.3.received = f32[136,16,128]{2,1,0:T(8,128)S(1)} collective-permute-done((f32[136,16,128]{2,1,0:T(8,128)S(1)}, f32[136,16,128]{2,1,0:T(8,128)S(1)}, u32[]{:S(2)}, u32[]{:S(2)}) %collective-permute-start.3) | collective-permute-done | bytes 1114144 | tf_op jit(solution)/shard_map/ppermute | solution.py:230
  152.0 15.4 %all_to_all.62 = f16[136,16,128]{2,1,0:T(8,128)(2,1)S(1)} all-to-all(f16[136,16,128]{2,1,0:T(8,128)(2,1)S(1)} %convert_element_type.36), channel_id=1, replica_groups=mesh['z'=4,'xl'=2,'xh'=2,'y'=4,'c'=2] {'xh','y'}, dimensions={0} | all-to-all | bytes 1114112 | tf_op jit(solution)/shard_map/all_to_all | solution.py:222
  167.5 1.0 shard_map.78
  168.4 14.2 %all_to_all.63.left_own = bf16[136,16,128]{2,1,0:T(8,128)(2,1)S(1)} all-to-all(bf16[136,16,128]{2,1,0:T(8,128)(2,1)S(1)} %get-tuple-element.42), channel_id=1, replica_groups=mesh['z'=4,'xl'=2,'xh'=2,'y'=4,'c'=2] {'xh','y'}, dimensions={0} | all-to-all | bytes 1114112 | tf_op jit(solution)/shard_map/all_to_all | solution.py:222
  182.7 2.0 collective-permute-done.4.left_other
  184.6 1.8 shard_map.79
  186.6 19.9 %all_to_all.64 = f16[264,16,128]{2,1,0:T(8,128)(2,1)S(1)} all-to-all(f16[264,16,128]{2,1,0:T(8,128)(2,1)S(1)} %convert_element_type.38), channel_id=1, replica_groups=mesh['z'=4,'xl'=2,'xh'=2,'y'=4,'c'=2] {'z','xl'}, dimensions={0} | all-to-all | bytes 2162688 | tf_op jit(solution)/shard_map/all_to_all | solution.py:222
  206.7 0.4 shard_map.80
  207.1 1.1 collective-permute-done.5
  208.3 14.1 %all_to_all.65.sums = f32[64,1,128]{2,1,0:T(1,128)S(1)} all-to-all(f32[64,1,128]{2,1,0:T(1,128)S(1)} %broadcast_in_dim.3), channel_id=1, replica_groups=mesh['z'=4,'xl'=2,'xh'=2,'y'=4,'c'=2] {'z','xl','xh','y'}, dimensions={0} | all-to-all | bytes 65536 | tf_op jit(solution)/shard_map/all_to_all | solution.py:222
  222.6 1.0 copy.7
  223.6 1.0 copy.8
  (33 shorter events, 1.9 us)
Async XLA Ops:
  0.6 0.9 copy-start.1
  1.5 21.0 %copy-start.2 = (s32[1,1,192]{2,1,0:T(1,128)S(1)}, s32[1,1,192]{2,1,0:T(1,128)}, u32[]{:S(2)}) copy-start(s32[1,1,192]{2,1,0:T(1,128)} %param.6) | copy-start | bytes 2308
  1.5 21.0 %copy-start.3 = (s32[1,1,192]{2,1,0:T(1,128)S(1)}, s32[1,1,192]{2,1,0:T(1,128)}, u32[]{:S(2)}) copy-start(s32[1,1,192]{2,1,0:T(1,128)} %param.7) | copy-start | bytes 2308
  20.6 2.0 collective-permute-start
  22.6 2.8 %copy-start = (bf16[1,1,192,128,128]{4,3,2,1,0:T(8,128)(2,1)S(1)}, bf16[1,1,192,128,128]{4,3,2,1,0:T(8,128)(2,1)}, u32[]{:S(2)}) copy-start(bf16[1,1,192,128,128]{4,3,2,1,0:T(8,128)(2,1)} %param.5) | copy-start | bytes 18874372
  69.1 36.9 %slice-start = ((s8[6291456]{0:T(1024)(128)(4,1)}), s8[4194304]{0:T(1024)(128)(4,1)S(1)}, s32[]{:S(2)}) async-start(s8[6291456]{0:T(1024)(128)(4,1)} %bitcast.11), calls=%async_computation.11 | async-start | bytes 8388608
  71.0 2.8 %collective-permute-start.1 = (f32[136,16,128]{2,1,0:T(8,128)S(1)}, f32[136,16,128]{2,1,0:T(8,128)S(1)}, u32[]{:S(2)}, u32[]{:S(2)}) collective-permute-start(f32[136,16,128]{2,1,0:T(8,128)S(1)} %get-tuple-element.31), channel_id=1, source_target_pairs={{0,1},{1,0},{2,3},{3,2},{4,5},{5,4},{6,7},{7,6},{8,9},{9,8},{10,11... | collective-permute-start | bytes 3342344 | tf_op jit(solution)/shard_map/ppermute | solution.py:230
  73.8 32.1 %slice-start.1 = ((s8[6291456]{0:T(1024)(128)(4,1)}), s8[2097152]{0:T(1024)(128)(4,1)S(1)}, s32[]{:S(2)}) async-start(s8[6291456]{0:T(1024)(128)(4,1)} %bitcast.11), calls=%async_computation.12 | async-start | bytes 4194304
  104.0 2.0 collective-permute-start.2
  149.0 2.8 %collective-permute-start.3 = (f32[136,16,128]{2,1,0:T(8,128)S(1)}, f32[136,16,128]{2,1,0:T(8,128)S(1)}, u32[]{:S(2)}, u32[]{:S(2)}) collective-permute-start(f32[136,16,128]{2,1,0:T(8,128)S(1)} %get-tuple-element.39), channel_id=1, source_target_pairs={{0,1},{1,0},{2,3},{3,2},{4,5},{5,4},{6,7},{7,6},{8,9},{9,8},{10,11... | collective-permute-start | bytes 3342344 | tf_op jit(solution)/shard_map/ppermute | solution.py:230
  182.7 2.0 collective-permute-start.4
  207.1 1.2 collective-permute-start.5

commit v3 on v2

--- a/solution.py
+++ b/solution.py
@@ -13,6 +13,8 @@
 CELL_GAIN = 4096.0
 RAY_GAIN = 2048.0
 CHUNK = 64
+FIRST_CHUNK = 32
+STAGGER = 7000
 CHIPS_OF_COL = ("xh", "y")
 DEVICES_OF_ROW = ("z", "xl")
 VMEM_BYTES = 32 << 20
@@ -33,10 +35,14 @@
     return side_lanes(lane, exponent, upper, fraction * 1024.0 - upper), exponent
 
 
-def pair_products(count, vector, held, source, visit):
+def pair_products(count, vector, held, source, visit, width=CHUNK, arrive=None):
+    chunks = (count + (width - 1)) // width
+
     def chunk(at, carry):
-        for step in range(0, CHUNK, 2):
-            slot = at * CHUNK + step
+        if arrive is not None:
+            arrive(at)
+        for step in range(0, width, 2):
+            slot = at * width + step
             picked = jnp.concatenate([vector[source(slot)], vector[source(slot + 1)]], axis=0)
             pair = jnp.concatenate([held[slot], held[slot + 1]], axis=1)
             both = lax.dot_general(picked, pair, (((1,), (0,)), ((), ())), preferred_element_type=jnp.float32)
@@ -45,7 +51,8 @@
             visit(slot + 1, both[rhs:, LANES:])
         return carry
 
-    lax.fori_loop(0, (count + (CHUNK - 1)) // CHUNK, chunk, 0)
+    lax.fori_loop(0, chunks, chunk, 0)
+    return chunks
 
 
 def rays_kernel(rows, cols, scalars, right, turned, keep, send, total):
@@ -72,10 +79,26 @@
     send[...] = total[half:]
 
 
-def cells_kernel(turn, rows, cols, scalars, left_own, left_other, held, out, *rest):
-    left = rest[-1]
+def cells_kernel(first, stagger, rows, cols, scalars, left_own, left_other, blocks, out, *rest):
     count, core = scalars[0], scalars[1]
     half = left_own.shape[0]
+    arrive, width = None, CHUNK
+    if first:
+        turned, held, left, sems = rest
+        width = FIRST_CHUNK
+        pieces = held.shape[0] // width
+
+        def fetch(at):
+            piece = pl.ds(at * width, width)
+            return pltpu.make_async_copy(blocks.at[piece], held.at[piece], sems.at[at])
+
+        def arrive(at):
+            fetch(at).wait()
+
+        for at in range(pieces):
+            fetch(at).start()
+    else:
+        held, (left,) = blocks, rest
     left[pl.ds(core * half, half)] = left_own[...]
     left[pl.ds((1 - core) * half, half)] = left_other[...]
     out[...] = jnp.zeros_like(out)
@@ -93,12 +116,24 @@
         col = cols[slot]
         place = jnp.where(slot < count, col + (col >> 5), 32)
         out[place] += product * scale
-        if turn:
-            rest[0][slot] = held[slot].T
-
-    pair_products(count, left, held, source, visit)
+        if first:
+            turned[slot] = held[slot].T
+
+    chunks = pair_products(count, left, held, source, visit, width, arrive)
+    if first:
+
+        def drain(at, carry):
+            arrive(at)
+            return carry
+
+        lax.fori_loop(chunks, pieces, drain, 0)
     for at in range(8):
         out[33 * at + 32] = packed
+    if stagger:
+
+        @pl.when(core == 1)
+        def _():
+            pl.delay(stagger)
 
 
 def send_blocks(sent, values, squares):
@@ -187,8 +222,8 @@
         direction0 = raw0[at] * over0
         direction1 = raw1[at] * over1 - turn1 * direction0
         direction2 = raw2[at] * over2 - turn2 * direction1
-        solution_out[:, lanes] = step1 * direction0 + step2 * direction1
-        scaled_out[:, lanes] = phi_bar * direction2
+        solution_out[:, 0, 0, lanes] = step1 * direction0 + step2 * direction1
+        scaled_out[:, 0, 0, lanes] = phi_bar * direction2
 
 
 def small_call(body, outs, *args):
@@ -201,16 +236,17 @@
     )(*args)
 
 
-def kernel_call(body, outs, scratch, tables, vectors, blocks):
+def kernel_call(body, outs, scratch, tables, vectors, blocks, place=pltpu.VMEM):
     specs = [pl.BlockSpec(memory_space=pltpu.SMEM)] * 3
-    specs += [pl.BlockSpec(memory_space=pltpu.VMEM)] * (len(vectors) + 1)
+    specs += [pl.BlockSpec(memory_space=pltpu.VMEM)] * len(vectors)
+    specs += [pl.BlockSpec(memory_space=place)]
     slots = blocks.shape[0]
     return pl.pallas_call(
         body,
         out_shape=outs,
         in_specs=specs,
         out_specs=[pl.BlockSpec(memory_space=pltpu.VMEM)] * len(outs),
-        scratch_shapes=[scratch],
+        scratch_shapes=scratch,
         compiler_params=pltpu.CompilerParams(vmem_limit_bytes=VMEM_BYTES),
         cost_estimate=pl.CostEstimate(
             flops=2 * slots * LANES * LANES * 16, bytes_accessed=slots * LANES * LANES * 2 + (4 << 20), transcendentals=0
@@ -257,7 +293,7 @@
         keep, send = kernel_call(
             rays_kernel,
             [shape((8 * 17,) + block, jnp.float32)] * 2,
-            pltpu.VMEM((16 * 17,) + block, jnp.float32),
+            [pltpu.VMEM((16 * 17,) + block, jnp.float32)],
             tables, (right_full,), turned,
         )
         (both,) = small_call(core_kernel, [shape((8 * 17,) + block, jnp.float32)], keep, swap_cores(send))
@@ -265,33 +301,33 @@
         outs = [shape((16,) + block, jnp.float32), one, rays_sent]
         return small_call(functools.partial(update_kernel, RAY_GAIN, False, False), outs, got, left_raw, beta)
 
-    def cells_of(sent, *previous, last=False):
+    def cells_of(sent, held, *previous, last=False):
         first = not previous
         left_own = exchange(sent, CHIPS_OF_COL)
         outs = [shape((8 * 33,) + block, jnp.float32)]
+        scratch = [pltpu.VMEM((16 * 17,) + block, jnp.bfloat16)]
         if first:
-            outs.append(shape(blocks_here.shape, blocks_here.dtype))
-        out, *turned = kernel_call(
-            functools.partial(cells_kernel, first),
-            outs,
-            pltpu.VMEM((16 * 17,) + block, jnp.bfloat16),
-            tables, (left_own, swap_cores(left_own)), blocks_here,
+            outs += [shape(held.shape, held.dtype)] * 2
+            scratch += [pltpu.SemaphoreType.DMA((held.shape[0] // FIRST_CHUNK,))]
+        out, *kept = kernel_call(
+            functools.partial(cells_kernel, first, 0 if last else STAGGER),
+            outs, scratch, tables, (left_own, swap_cores(left_own)), held,
+            pltpu.HBM if first else pltpu.VMEM,
         )
         got = exchange_halves(out, DEVICES_OF_ROW)
         outs = [shape((32,) + block, jnp.float32), one, shape((1, LANES), jnp.float32) if last else cells_sent]
-        return (*small_call(functools.partial(update_kernel, CELL_GAIN, first, last), outs, got, *previous), *turned)
+        return (*small_call(functools.partial(update_kernel, CELL_GAIN, first, last), outs, got, *previous), *kept)
 
     sent, left_raw = small_call(start_kernel, [rays_sent, shape((16,) + block, jnp.float32)], travel_times)
-    raw0, beta0, sent, turned = cells_of(sent)
+    raw0, beta0, sent, turned, held = cells_of(sent, pltpu.with_memory_space_constraint(blocks_here, pltpu.HBM))
     left_raw, alpha0, sent = rays_of(sent, turned, left_raw, beta0)
-    raw1, beta1, sent = cells_of(sent, raw0, alpha0)
+    raw1, beta1, sent = cells_of(sent, held, raw0, alpha0)
     left_raw, alpha1, sent = rays_of(sent, turned, left_raw, beta1)
-    raw2, beta2, squares = cells_of(sent, raw1, alpha1, last=True)
+    raw2, beta2, squares = cells_of(sent, held, raw1, alpha1, last=True)
     squares = squares + swap_cores(squares)
     sums = exchange(jnp.broadcast_to(squares, (64, 1, LANES)), DEVICES_OF_ROW + CHIPS_OF_COL)
-    flat = shape((count_rhs, 32 * LANES), jnp.float32)
-    outs = small_call(finish_kernel, [flat] * 2, sums, raw0, raw1, raw2, alpha0, alpha1, beta0, beta1, beta2)
-    return tuple(out.reshape(count_rhs, 1, 1, -1) for out in outs)
+    flat = shape((count_rhs, 1, 1, 32 * LANES), jnp.float32)
+    return small_call(finish_kernel, [flat] * 2, sums, raw0, raw1, raw2, alpha0, alpha1, beta0, beta1, beta2)
 
 
 def solution(mesh):

time: 225 us -> 216 us (0.960)
  blocking collectives: 191 us -> 176 us
  starting transfers between devices: 0.19 us -> 10.4 us
  local copies, waits for them, and re-layouts: 5.66 us -> 0.93 us
  Pallas kernels: 12.7 us -> 15.2 us
    all_to_all x11, blocking collectives: 191 us -> 176 us  [exchange(): return lax.all_to_all(sent, axes, 0, 0, tiled=True)]
    ppermute x6, starting transfers between devices: 0.19 us -> 10.4 us  [swap_cores(): return lax.ppermute(values, 'c', [(0, 1), (1, 0)])]
    unnamed x14 -> x6, local copies, waits for them, and re-layouts: 5.64 us -> 0.9 us
where the time goes in v3:
time: 216 us
  blocking collectives  176 us (81%)
  Pallas kernels  15.2 us (7%)
  waiting for transfers between devices  11 us (5%)
  starting transfers between devices  10.4 us (5%)
    all_to_all x11, blocking collectives, exchange(): return lax.all_to_all(sent, axes, 0, 0, tiled=True)  176 us
    ppermute x6, waiting for transfers between devices, swap_cores(): return lax.ppermute(values, 'c', [(0, 1), (1, 0)])  11 us
    pallas_call x5, Pallas kernels, kernel_call(): pl.pallas_call(body, out_shape=outs, in_specs=specs, out_specs=[pl.BlockS...  10.9 us
    ppermute x6, starting transfers between devices, swap_cores(): return lax.ppermute(values, 'c', [(0, 1), (1, 0)])  10.4 us
    pallas_call x9, Pallas kernels, small_call(): pl.pallas_call(body, out_shape=outs, in_specs=[pl.BlockSpec(memory_space=...  4.35 us
  transfers between devices with their start and end apart: 6, of which 6 were waited for; matrix products, arithmetic and copies ran while one was open for 0% of the time, Pallas kernels for 0%

profile of v3, /device:TPU:0, one launch (start us, length us, event | category | flops | bytes accessed | tf_op | source)
XLA Modules:
  0.0 216.1 jit_solution(8113988771625988394)
XLA Ops:
  0.6 0.9 copy-done
  1.6 19.0 %all_to_all.55.left_own = bf16[136,16,128]{2,1,0:T(8,128)(2,1)S(1)} all-to-all(bf16[136,16,128]{2,1,0:T(8,128)(2,1)S(1)} %get-tuple-element.25), channel_id=1, replica_groups=mesh['z'=4,'xl'=2,'xh'=2,'y'=4,'c'=2] {'xh','y'}, dimensions={0} | all-to-all | bytes 1114112 | tf_op jit(solution)/shard_map/all_to_all | solution.py:258
  21.3 1.2 collective-permute-done.left_other
  22.6 3.5 %shard_map.69 = (f32[264,16,128]{2,1,0:T(8,128)S(1)}, bf16[192,128,128]{2,1,0:T(8,128)(2,1)S(1)}, bf16[192,128,128]{2,1,0:T(8,128)(2,1)S(1)}) custom-call(s32[192]{0:T(256)S(1)} %bitcast.8, s32[192]{0:T(256)S(1)} %bitcast.13, s32[2]{0:T(128)S(1)} %pad_add_fusion.scalars, bf16[136,16,128]{2,1,0:T(8,128)(2,1)S(1)} %all_to_all.55.left_own, ...), custom_call_target="tpu_custom_call" | custom-call | flops 100663296 | bytes 10485760 | tf_op jit(solution)/shard_map/pallas_call | solution.py:244
  26.2 17.4 %all_to_all.56 = f16[264,16,128]{2,1,0:T(8,128)(2,1)S(1)} all-to-all(f16[264,16,128]{2,1,0:T(8,128)(2,1)S(1)} %convert_element_type.30), channel_id=1, replica_groups=mesh['z'=4,'xl'=2,'xh'=2,'y'=4,'c'=2] {'z','xl'}, dimensions={0} | all-to-all | bytes 2162688 | tf_op jit(solution)/shard_map/all_to_all | solution.py:258
  43.6 0.2 convert_element_type.31.got
  43.8 0.4 shard_map.70
  44.2 15.5 %all_to_all.57.right = bf16[264,16,128]{2,1,0:T(8,128)(2,1)S(1)} all-to-all(bf16[264,16,128]{2,1,0:T(8,128)(2,1)S(1)} %get-tuple-element.27), channel_id=1, replica_groups=mesh['z'=4,'xl'=2,'xh'=2,'y'=4,'c'=2] {'z','xl'}, dimensions={0} | all-to-all | bytes 2162688 | tf_op jit(solution)/shard_map/all_to_all | solution.py:258
  59.8 1.9 shard_map.71
  61.6 5.1 %collective-permute-start.1 = (f32[136,16,128]{2,1,0:T(8,128)S(1)}, f32[136,16,128]{2,1,0:T(8,128)S(1)}, u32[]{:S(2)}, u32[]{:S(2)}) collective-permute-start(f32[136,16,128]{2,1,0:T(8,128)S(1)} %get-tuple-element.30), channel_id=1, source_target_pairs={{0,1},{1,0},{2,3},{3,2},{4,5},{5,4},{6,7},{7,6},{8,9},{9,8},{10,11... | collective-permute-start | bytes 3342344 | tf_op jit(solution)/shard_map/ppermute | solution.py:266
  66.7 2.4 %collective-permute-done.1.received = f32[136,16,128]{2,1,0:T(8,128)S(1)} collective-permute-done((f32[136,16,128]{2,1,0:T(8,128)S(1)}, f32[136,16,128]{2,1,0:T(8,128)S(1)}, u32[]{:S(2)}, u32[]{:S(2)}) %collective-permute-start.1) | collective-permute-done | bytes 1114144 | tf_op jit(solution)/shard_map/ppermute | solution.py:266
  69.3 15.8 %all_to_all.58 = f16[136,16,128]{2,1,0:T(8,128)(2,1)S(1)} all-to-all(f16[136,16,128]{2,1,0:T(8,128)(2,1)S(1)} %convert_element_type.32), channel_id=1, replica_groups=mesh['z'=4,'xl'=2,'xh'=2,'y'=4,'c'=2] {'xh','y'}, dimensions={0} | all-to-all | bytes 1114112 | tf_op jit(solution)/shard_map/all_to_all | solution.py:258
  85.2 0.4 shard_map.73
  85.6 14.5 %all_to_all.59.left_own = bf16[136,16,128]{2,1,0:T(8,128)(2,1)S(1)} all-to-all(bf16[136,16,128]{2,1,0:T(8,128)(2,1)S(1)} %get-tuple-element.33), channel_id=1, replica_groups=mesh['z'=4,'xl'=2,'xh'=2,'y'=4,'c'=2] {'xh','y'}, dimensions={0} | all-to-all | bytes 1114112 | tf_op jit(solution)/shard_map/all_to_all | solution.py:258
  100.1 2.0 collective-permute-done.2.left_other
  102.0 1.8 shard_map.74
  104.0 14.7 %all_to_all.60 = f16[264,16,128]{2,1,0:T(8,128)(2,1)S(1)} all-to-all(f16[264,16,128]{2,1,0:T(8,128)(2,1)S(1)} %convert_element_type.34), channel_id=1, replica_groups=mesh['z'=4,'xl'=2,'xh'=2,'y'=4,'c'=2] {'z','xl'}, dimensions={0} | all-to-all | bytes 2162688 | tf_op jit(solution)/shard_map/all_to_all | solution.py:258
  118.9 0.4 shard_map.75
  119.3 15.3 %all_to_all.61.right = bf16[264,16,128]{2,1,0:T(8,128)(2,1)S(1)} all-to-all(bf16[264,16,128]{2,1,0:T(8,128)(2,1)S(1)} %get-tuple-element.37), channel_id=1, replica_groups=mesh['z'=4,'xl'=2,'xh'=2,'y'=4,'c'=2] {'z','xl'}, dimensions={0} | all-to-all | bytes 2162688 | tf_op jit(solution)/shard_map/all_to_all | solution.py:258
  134.7 1.9 shard_map.76
  136.6 5.3 %collective-permute-start.3 = (f32[136,16,128]{2,1,0:T(8,128)S(1)}, f32[136,16,128]{2,1,0:T(8,128)S(1)}, u32[]{:S(2)}, u32[]{:S(2)}) collective-permute-start(f32[136,16,128]{2,1,0:T(8,128)S(1)} %get-tuple-element.39), channel_id=1, source_target_pairs={{0,1},{1,0},{2,3},{3,2},{4,5},{5,4},{6,7},{7,6},{8,9},{9,8},{10,11... | collective-permute-start | bytes 3342344 | tf_op jit(solution)/shard_map/ppermute | solution.py:266
  141.8 2.4 %collective-permute-done.3.received = f32[136,16,128]{2,1,0:T(8,128)S(1)} collective-permute-done((f32[136,16,128]{2,1,0:T(8,128)S(1)}, f32[136,16,128]{2,1,0:T(8,128)S(1)}, u32[]{:S(2)}, u32[]{:S(2)}) %collective-permute-start.3) | collective-permute-done | bytes 1114144 | tf_op jit(solution)/shard_map/ppermute | solution.py:266
  144.4 15.3 %all_to_all.62 = f16[136,16,128]{2,1,0:T(8,128)(2,1)S(1)} all-to-all(f16[136,16,128]{2,1,0:T(8,128)(2,1)S(1)} %convert_element_type.36), channel_id=1, replica_groups=mesh['z'=4,'xl'=2,'xh'=2,'y'=4,'c'=2] {'xh','y'}, dimensions={0} | all-to-all | bytes 1114112 | tf_op jit(solution)/shard_map/all_to_all | solution.py:258
  159.9 1.0 shard_map.78
  160.8 14.6 %all_to_all.63.left_own = bf16[136,16,128]{2,1,0:T(8,128)(2,1)S(1)} all-to-all(bf16[136,16,128]{2,1,0:T(8,128)(2,1)S(1)} %get-tuple-element.42), channel_id=1, replica_groups=mesh['z'=4,'xl'=2,'xh'=2,'y'=4,'c'=2] {'xh','y'}, dimensions={0} | all-to-all | bytes 1114112 | tf_op jit(solution)/shard_map/all_to_all | solution.py:258
  175.4 2.0 collective-permute-done.4.left_other
  177.3 1.8 shard_map.79
  179.3 19.7 %all_to_all.64 = f16[264,16,128]{2,1,0:T(8,128)(2,1)S(1)} all-to-all(f16[264,16,128]{2,1,0:T(8,128)(2,1)S(1)} %convert_element_type.38), channel_id=1, replica_groups=mesh['z'=4,'xl'=2,'xh'=2,'y'=4,'c'=2] {'z','xl'}, dimensions={0} | all-to-all | bytes 2162688 | tf_op jit(solution)/shard_map/all_to_all | solution.py:258
  199.2 0.4 shard_map.80
  199.7 1.1 collective-permute-done.5
  200.8 13.9 %all_to_all.65.sums = f32[64,1,128]{2,1,0:T(1,128)S(1)} all-to-all(f32[64,1,128]{2,1,0:T(1,128)S(1)} %broadcast_in_dim.3), channel_id=1, replica_groups=mesh['z'=4,'xl'=2,'xh'=2,'y'=4,'c'=2] {'z','xl','xh','y'}, dimensions={0} | all-to-all | bytes 65536 | tf_op jit(solution)/shard_map/all_to_all | solution.py:258
  214.7 1.4 shard_map.81
  (24 shorter events, 1.5 us)
Async XLA Ops:
  0.6 0.9 copy-start
  1.5 21.0 %copy-start.1 = (s32[1,1,192]{2,1,0:T(1,128)S(1)}, s32[1,1,192]{2,1,0:T(1,128)}, u32[]{:S(2)}) copy-start(s32[1,1,192]{2,1,0:T(1,128)} %param.6) | copy-start | bytes 2308
  1.5 21.0 %copy-start.2 = (s32[1,1,192]{2,1,0:T(1,128)S(1)}, s32[1,1,192]{2,1,0:T(1,128)}, u32[]{:S(2)}) copy-start(s32[1,1,192]{2,1,0:T(1,128)} %param.7) | copy-start | bytes 2308
  20.6 2.0 collective-permute-start
  61.6 7.5 %collective-permute-start.1 = (f32[136,16,128]{2,1,0:T(8,128)S(1)}, f32[136,16,128]{2,1,0:T(8,128)S(1)}, u32[]{:S(2)}, u32[]{:S(2)}) collective-permute-start(f32[136,16,128]{2,1,0:T(8,128)S(1)} %get-tuple-element.30), channel_id=1, source_target_pairs={{0,1},{1,0},{2,3},{3,2},{4,5},{5,4},{6,7},{7,6},{8,9},{9,8},{10,11... | collective-permute-start | bytes 3342344 | tf_op jit(solution)/shard_map/ppermute | solution.py:266
  100.0 2.0 collective-permute-start.2
  136.6 7.7 %collective-permute-start.3 = (f32[136,16,128]{2,1,0:T(8,128)S(1)}, f32[136,16,128]{2,1,0:T(8,128)S(1)}, u32[]{:S(2)}, u32[]{:S(2)}) collective-permute-start(f32[136,16,128]{2,1,0:T(8,128)S(1)} %get-tuple-element.39), channel_id=1, source_target_pairs={{0,1},{1,0},{2,3},{3,2},{4,5},{5,4},{6,7},{7,6},{8,9},{9,8},{10,11... | collective-permute-start | bytes 3342344 | tf_op jit(solution)/shard_map/ppermute | solution.py:266
  175.4 2.0 collective-permute-start.4
  199.6 1.2 collective-permute-start.5

commit v4 on v3

--- a/solution.py
+++ b/solution.py
@@ -12,8 +12,10 @@
 SQUARES_FLOOR = 1e-30
 CELL_GAIN = 4096.0
 RAY_GAIN = 2048.0
-CHUNK = 64
+SLOTS = 192
+COUNTS = 2 * SLOTS
 FIRST_CHUNK = 32
+LIST_CHUNK = 32
 STAGGER = 7000
 CHIPS_OF_COL = ("xh", "y")
 DEVICES_OF_ROW = ("z", "xl")
@@ -35,7 +37,7 @@
     return side_lanes(lane, exponent, upper, fraction * 1024.0 - upper), exponent
 
 
-def pair_products(count, vector, held, source, visit, width=CHUNK, arrive=None):
+def pair_products(count, vector, held, source, visit, width, arrive, slot_of):
     chunks = (count + (width - 1)) // width
 
     def chunk(at, carry):
@@ -44,7 +46,7 @@
         for step in range(0, width, 2):
             slot = at * width + step
             picked = jnp.concatenate([vector[source(slot)], vector[source(slot + 1)]], axis=0)
-            pair = jnp.concatenate([held[slot], held[slot + 1]], axis=1)
+            pair = jnp.concatenate([held[slot_of(slot)], held[slot_of(slot + 1)]], axis=1)
             both = lax.dot_general(picked, pair, (((1,), (0,)), ((), ())), preferred_element_type=jnp.float32)
             rhs = both.shape[0] // 2
             visit(slot, both[:rhs, :LANES])
@@ -55,57 +57,105 @@
     return chunks
 
 
-def rays_kernel(rows, cols, scalars, right, turned, keep, send, total):
-    count, core = scalars[0], scalars[1]
-    half = keep.shape[0]
-    total[...] = jnp.zeros_like(total)
-    side = sum(right[33 * at + 32].astype(jnp.float32) for at in range(8))
-    squares = jnp.broadcast_to(jnp.sum(side, axis=1, keepdims=True), side.shape)
-
-    def source(slot):
-        col = cols[slot]
-        return col + (col >> 5)
-
-    def visit(slot, product):
-        row = rows[slot]
-        place = (((row >> 4) & 1) ^ core) * half + (row >> 5) * 17 + (row & 15)
-        place = jnp.where(slot < count, place, 16)
-        total[place] += product
-
-    pair_products(count, right, turned, source, visit)
-    for at in range(16):
-        total[17 * at + 16] = squares
-    keep[...] = total[:half]
-    send[...] = total[half:]
-
-
-def cells_kernel(first, stagger, rows, cols, scalars, left_own, left_other, blocks, out, *rest):
+def sum_of_sides(rows):
+    side = sum(row.astype(jnp.float32) for row in rows)
+    return jnp.broadcast_to(jnp.sum(side, axis=1, keepdims=True), side.shape)
+
+
+def listed(table, start, count, vector, held, source, place, spare, out):
+    def entry(at):
+        return jnp.where(at < count, table[start + at], 0)
+
+    def slot_of(at):
+        return entry(at) & 255
+
+    def visit(at, product):
+        out[jnp.where(at < count, place(entry(at)), spare)] += product
+
+    pair_products(count, vector, held, lambda at: source(entry(at)), visit, LIST_CHUNK, None, slot_of)
+
+
+def ray_place(entry):
+    row = entry >> 16
+    return (row >> 5) * 17 + (row & 15)
+
+
+def cell_place(entry):
+    col = (entry >> 8) & 255
+    return col + (col >> 5)
+
+
+def rays_kernel(other, table, right, turned, out):
+    out[...] = jnp.zeros_like(out)
+    squares = sum_of_sides([right[33 * at + 32] for at in range(8)])
+    start, count = (SLOTS, table[COUNTS + 1]) if other else (0, table[COUNTS])
+    listed(table, start, count, right, turned, cell_place, ray_place, 16, out)
+    if other:
+        packed, exponent = side_of_squares(squares, lax.broadcasted_iota(jnp.int32, squares.shape, 1))
+        scale = RAY_GAIN * jnp.exp2(-0.5 * exponent)
+        for at in range(out.shape[0]):
+            out[at] = out[at] * scale
+        squares = packed
+    out[16] = squares
+
+
+def own_cells_kernel(table, left, held, out):
+    out[...] = jnp.zeros_like(out)
+    listed(table, 0, table[COUNTS], left, held, ray_place, cell_place, 32, out)
+
+
+def other_cells_kernel(stagger, table, left_own, left, partial_out, held, out):
+    out[...] = partial_out[...]
+    listed(table, SLOTS, table[COUNTS + 1], left, held, ray_place, cell_place, 32, out)
+    squares = sum_of_sides([half[17 * at + 16] for half in (left_own, left) for at in range(8)])
+    packed, exponent = side_of_squares(squares, lax.broadcasted_iota(jnp.int32, squares.shape, 1))
+    scale = CELL_GAIN * jnp.exp2(-0.5 * exponent)
+    for at in range(out.shape[0]):
+        out[at] = packed if at % 33 == 32 else out[at] * scale
+    if stagger:
+
+        @pl.when(table[COUNTS + 2] == 1)
+        def _():
+            pl.delay(stagger)
+
+
+def first_cells_kernel(stagger, rows, cols, scalars, left_own, left_other, blocks, out, turned, held, table, left, sems):
     count, core = scalars[0], scalars[1]
     half = left_own.shape[0]
-    arrive, width = None, CHUNK
-    if first:
-        turned, held, left, sems = rest
-        width = FIRST_CHUNK
-        pieces = held.shape[0] // width
-
-        def fetch(at):
-            piece = pl.ds(at * width, width)
-            return pltpu.make_async_copy(blocks.at[piece], held.at[piece], sems.at[at])
-
-        def arrive(at):
-            fetch(at).wait()
-
-        for at in range(pieces):
-            fetch(at).start()
-    else:
-        held, (left,) = blocks, rest
+    pieces = held.shape[0] // FIRST_CHUNK
+
+    def fetch(at):
+        piece = pl.ds(at * FIRST_CHUNK, FIRST_CHUNK)
+        return pltpu.make_async_copy(blocks.at[piece], held.at[piece], sems.at[at])
+
+    def arrive(at):
+        fetch(at).wait()
+
+    for at in range(pieces):
+        fetch(at).start()
+
+    def enlist(group, counts):
+        own, other = counts
+        for step in range(8):
+            slot = group * 8 + step
+            row = rows[slot]
+            filled = jnp.where(slot < count, 1, 0)
+            mine = jnp.where(((row >> 4) & 1) == core, filled, 0)
+            place = jnp.where(filled == 1, jnp.where(mine == 1, own, SLOTS + other), COUNTS + 3)
+            table[place] = slot | (cols[slot] << 8) | (row << 16)
+            own, other = own + mine, other + filled - mine
+        return own, other
+
+    own, other = lax.fori_loop(0, SLOTS // 8, enlist, (jnp.int32(0), jnp.int32(0)))
+    table[COUNTS] = own
+    table[COUNTS + 1] = other
+    table[COUNTS + 2] = core
+
     left[pl.ds(core * half, half)] = left_own[...]
     left[pl.ds((1 - core) * half, half)] = left_other[...]
     out[...] = jnp.zeros_like(out)
-    side = sum(left[17 * at + 16].astype(jnp.float32) for at in range(16))
-    squares = jnp.broadcast_to(jnp.sum(side, axis=1, keepdims=True), side.shape)
-    lane = lax.broadcasted_iota(jnp.int32, side.shape, 1)
-    packed, exponent = side_of_squares(squares, lane)
+    squares = sum_of_sides([left[17 * at + 16] for at in range(16)])
+    packed, exponent = side_of_squares(squares, lax.broadcasted_iota(jnp.int32, squares.shape, 1))
     scale = CELL_GAIN * jnp.exp2(-0.5 * exponent)
 
     def source(slot):
@@ -116,17 +166,15 @@
         col = cols[slot]
         place = jnp.where(slot < count, col + (col >> 5), 32)
         out[place] += product * scale
-        if first:
-            turned[slot] = held[slot].T
-
-    chunks = pair_products(count, left, held, source, visit, width, arrive)
-    if first:
-
-        def drain(at, carry):
-            arrive(at)
-            return carry
-
-        lax.fori_loop(chunks, pieces, drain, 0)
+        turned[slot] = held[slot].T
+
+    chunks = pair_products(count, left, held, source, visit, FIRST_CHUNK, arrive, lambda slot: slot)
+
+    def drain(at, carry):
+        arrive(at)
+        return carry
+
+    lax.fori_loop(chunks, pieces, drain, 0)
     for at in range(8):
         out[33 * at + 32] = packed
     if stagger:
@@ -161,18 +209,21 @@
 
 
 def core_kernel(keep, received, out):
-    squares = keep[16] + received[16]
-    lane = lax.broadcasted_iota(jnp.int32, squares.shape, 1)
-    packed, exponent = side_of_squares(squares, lane)
+    side = received[16]
+    exponent = side[:, 0:1]
+    squares = keep[16] + (side[:, 1:2] + side[:, 2:3]) * (1.0 / 1024.0) * jnp.exp2(exponent)
+    weight = jnp.broadcast_to(jnp.exp2(0.5 * exponent) * (1.0 / RAY_GAIN), squares.shape)
+    packed, exponent = side_of_squares(squares, lax.broadcasted_iota(jnp.int32, squares.shape, 1))
     scale = RAY_GAIN * jnp.exp2(-0.5 * exponent)
+    weight = weight * scale
     for chip in range(8):
-        for at in range(16):
-            out[17 * chip + at] = (keep[17 * chip + at] + received[17 * chip + at]) * scale
+        for at in range(17 * chip, 17 * chip + 16):
+            out[at] = keep[at] * scale + received[at] * weight
         out[17 * chip + 16] = packed
 
 
 def update_kernel(gain, first, last, got, *rest):
-    previous, (raw, norm_out, tail) = rest[:-3], rest[-3:]
+    previous, (norm_out, tail, raw) = rest[:-3], rest[-3:]
     size = raw.shape[0] + 1
     weights, total = [], 0.0
     for source in range(8):
@@ -226,32 +277,31 @@
         scaled_out[:, 0, 0, lanes] = phi_bar * direction2
 
 
-def small_call(body, outs, *args):
+def small_call(body, outs, *args, scratch=()):
     return pl.pallas_call(
         body,
         out_shape=outs,
         in_specs=[pl.BlockSpec(memory_space=pltpu.VMEM)] * len(args),
         out_specs=[pl.BlockSpec(memory_space=pltpu.VMEM)] * len(outs),
+        scratch_shapes=scratch,
         compiler_params=pltpu.CompilerParams(vmem_limit_bytes=VMEM_BYTES),
     )(*args)
 
 
-def kernel_call(body, outs, scratch, tables, vectors, blocks, place=pltpu.VMEM):
-    specs = [pl.BlockSpec(memory_space=pltpu.SMEM)] * 3
-    specs += [pl.BlockSpec(memory_space=pltpu.VMEM)] * len(vectors)
-    specs += [pl.BlockSpec(memory_space=place)]
-    slots = blocks.shape[0]
+def kernel_call(body, outs, scalars, *operands, scratch=(), in_hbm=False):
+    specs = [pl.BlockSpec(memory_space=pltpu.SMEM)] * len(scalars)
+    specs += [pl.BlockSpec(memory_space=pltpu.VMEM)] * (len(operands) - 1)
+    specs += [pl.BlockSpec(memory_space=pltpu.HBM if in_hbm else pltpu.VMEM)]
+    places = [pltpu.SMEM if out.dtype == jnp.int32 else pltpu.VMEM for out in outs]
     return pl.pallas_call(
         body,
         out_shape=outs,
         in_specs=specs,
-        out_specs=[pl.BlockSpec(memory_space=pltpu.VMEM)] * len(outs),
+        out_specs=[pl.BlockSpec(memory_space=place) for place in places],
         scratch_shapes=scratch,
         compiler_params=pltpu.CompilerParams(vmem_limit_bytes=VMEM_BYTES),
-        cost_estimate=pl.CostEstimate(
-            flops=2 * slots * LANES * LANES * 16, bytes_accessed=slots * LANES * LANES * 2 + (4 << 20), transcendentals=0
-        ),
-    )(*tables, *vectors, blocks)
+        cost_estimate=pl.CostEstimate(flops=10**9, bytes_accessed=4 << 20, transcendentals=0),
+    )(*scalars, *operands)
 
 
 def exchange(sent, axes):
@@ -288,42 +338,55 @@
     cells_sent = shape((8 * 33,) + block, jnp.bfloat16)
     one = shape(block, jnp.float32)
 
-    def rays_of(sent, turned, left_raw, beta):
-        right_full = exchange(sent, DEVICES_OF_ROW)
-        keep, send = kernel_call(
-            rays_kernel,
-            [shape((8 * 17,) + block, jnp.float32)] * 2,
-            [pltpu.VMEM((16 * 17,) + block, jnp.float32)],
-            tables, (right_full,), turned,
-        )
-        (both,) = small_call(core_kernel, [shape((8 * 17,) + block, jnp.float32)], keep, swap_cores(send))
+    rays_part = [shape((8 * 17,) + block, jnp.float32)]
+    cells_part = [shape((8 * 33,) + block, jnp.float32)]
+
+    def rays_of(sent, table, turned, left_raw, beta, last=False):
+        right = exchange(sent, DEVICES_OF_ROW)
+        (send,) = kernel_call(functools.partial(rays_kernel, True), rays_part, [table], right, turned)
+        received = swap_cores(send.astype(jnp.float16))
+        (keep,) = kernel_call(functools.partial(rays_kernel, False), rays_part, [table], right, turned)
+        (both,) = small_call(core_kernel, rays_part, keep, received.astype(jnp.float32))
         got = exchange_halves(both, CHIPS_OF_COL)
-        outs = [shape((16,) + block, jnp.float32), one, rays_sent]
-        return small_call(functools.partial(update_kernel, RAY_GAIN, False, False), outs, got, left_raw, beta)
-
-    def cells_of(sent, held, *previous, last=False):
-        first = not previous
+        body = functools.partial(update_kernel, RAY_GAIN, False, False)
+        raw = shape((16,) + block, jnp.float32)
+        if last:
+            return small_call(body, [one, rays_sent], got, left_raw, beta, scratch=[pltpu.VMEM(raw.shape, raw.dtype)])
+        return small_call(body, [one, rays_sent, raw], got, left_raw, beta)
+
+    def cells_of(sent, table, held, *previous, last=False):
         left_own = exchange(sent, CHIPS_OF_COL)
-        outs = [shape((8 * 33,) + block, jnp.float32)]
-        scratch = [pltpu.VMEM((16 * 17,) + block, jnp.bfloat16)]
-        if first:
-            outs += [shape(held.shape, held.dtype)] * 2
-            scratch += [pltpu.SemaphoreType.DMA((held.shape[0] // FIRST_CHUNK,))]
-        out, *kept = kernel_call(
-            functools.partial(cells_kernel, first, 0 if last else STAGGER),
-            outs, scratch, tables, (left_own, swap_cores(left_own)), held,
-            pltpu.HBM if first else pltpu.VMEM,
+        left_other = swap_cores(left_own)
+        (out,) = kernel_call(own_cells_kernel, cells_part, [table], left_own, held)
+        body = functools.partial(other_cells_kernel, 0 if last else STAGGER)
+        (out,) = kernel_call(body, cells_part, [table], left_own, left_other, out, held)
+        got = exchange_halves(out, DEVICES_OF_ROW)
+        outs = [one, shape((1, LANES), jnp.float32) if last else cells_sent, shape((32,) + block, jnp.float32)]
+        return small_call(functools.partial(update_kernel, CELL_GAIN, False, last), outs, got, *previous)
+
+    def first_cells_of(sent):
+        left_own = exchange(sent, CHIPS_OF_COL)
+        outs = cells_part + [shape(blocks_here.shape, jnp.bfloat16)] * 2 + [shape((COUNTS + 16,), jnp.int32)]
+        scratch = [
+            pltpu.VMEM((16 * 17,) + block, jnp.bfloat16),
+            pltpu.SemaphoreType.DMA((SLOTS // FIRST_CHUNK,)),
+        ]
+        out, turned, held, table = kernel_call(
+            functools.partial(first_cells_kernel, STAGGER),
+            outs, tables, left_own, swap_cores(left_own),
+            pltpu.with_memory_space_constraint(blocks_here, pltpu.HBM),
+            scratch=scratch, in_hbm=True,
         )
         got = exchange_halves(out, DEVICES_OF_ROW)
-        outs = [shape((32,) + block, jnp.float32), one, shape((1, LANES), jnp.float32) if last else cells_sent]
-        return (*small_call(functools.partial(update_kernel, CELL_GAIN, first, last), outs, got, *previous), *kept)
+        outs = [one, cells_sent, shape((32,) + block, jnp.float32)]
+        return (*small_call(functools.partial(update_kernel, CELL_GAIN, True, False), outs, got), turned, held, table)
 
     sent, left_raw = small_call(start_kernel, [rays_sent, shape((16,) + block, jnp.float32)], travel_times)
-    raw0, beta0, sent, turned, held = cells_of(sent, pltpu.with_memory_space_constraint(blocks_here, pltpu.HBM))
-    left_raw, alpha0, sent = rays_of(sent, turned, left_raw, beta0)
-    raw1, beta1, sent = cells_of(sent, held, raw0, alpha0)
-    left_raw, alpha1, sent = rays_of(sent, turned, left_raw, beta1)
-    raw2, beta2, squares = cells_of(sent, held, raw1, alpha1, last=True)
+    beta0, sent, raw0, turned, held, table = first_cells_of(sent)
+    alpha0, sent, left_raw = rays_of(sent, table, turned, left_raw, beta0)
+    beta1, sent, raw1 = cells_of(sent, table, held, raw0, alpha0)
+    alpha1, sent = rays_of(sent, table, turned, left_raw, beta1, last=True)
+    beta2, squares, raw2 = cells_of(sent, table, held, raw1, alpha1, last=True)
     squares = squares + swap_cores(squares)
     sums = exchange(jnp.broadcast_to(squares, (64, 1, LANES)), DEVICES_OF_ROW + CHIPS_OF_COL)
     flat = shape((count_rhs, 1, 1, 32 * LANES), jnp.float32)

time: 216 us -> 214 us (level)
  waiting for transfers between devices: 11 us -> 4.14 us
  Pallas kernels: 15.2 us -> 19.8 us
    ppermute x6, waiting for transfers between devices: 11 us -> 4.14 us  [swap_cores(): return lax.ppermute(values, 'c', [(0, 1), (1, 0)])]
    pallas_call x5 -> x9, Pallas kernels: 10.9 us -> 15.7 us  [kernel_call(): pl.pallas_call(body, out_shape=outs, in_specs=specs, out_specs=[pl.BlockS...]
  transfers between devices with their start and end apart: 6 -> 6, of which waited for: 6 -> 6; matrix products, arithmetic and copies ran while one was open for 0% -> 0% of each run, Pallas kernels for 0% -> 2%
where the time goes in v4:
time: 214 us
  blocking collectives  175 us (82%)
  Pallas kernels  19.8 us (9%)
  starting transfers between devices  10.6 us (5%)
  waiting for transfers between devices  4.14 us (2%)
    all_to_all x11, blocking collectives, exchange(): return lax.all_to_all(sent, axes, 0, 0, tiled=True)  175 us
    pallas_call x9, Pallas kernels, kernel_call(): pl.pallas_call(body, out_shape=outs, in_specs=specs, out_specs=[pl.BlockS...  15.7 us
    ppermute x6, starting transfers between devices, swap_cores(): return lax.ppermute(values, 'c', [(0, 1), (1, 0)])  10.6 us
  transfers between devices with their start and end apart: 6, of which 6 were waited for; matrix products, arithmetic and copies ran while one was open for 0% of the time, Pallas kernels for 2%

profile of v4, /device:TPU:0, one launch (start us, length us, event | category | flops | bytes accessed | tf_op | source)
XLA Modules:
  0.0 213.6 jit_solution(5960520871741690050)
XLA Ops:
  0.6 0.9 copy-done
  1.6 19.0 %all_to_all.55.left_own = bf16[136,16,128]{2,1,0:T(8,128)(2,1)S(1)} all-to-all(bf16[136,16,128]{2,1,0:T(8,128)(2,1)S(1)} %get-tuple-element.22), channel_id=1, replica_groups=mesh['z'=4,'xl'=2,'xh'=2,'y'=4,'c'=2] {'xh','y'}, dimensions={0} | all-to-all | bytes 1114112 | tf_op jit(solution)/shard_map/all_to_all | solution.py:308
  21.3 1.2 collective-permute-done.left_other
  22.6 4.3 %shard_map.69 = (f32[264,16,128]{2,1,0:T(8,128)S(1)}, bf16[192,128,128]{2,1,0:T(8,128)(2,1)S(1)}, bf16[192,128,128]{2,1,0:T(8,128)(2,1)S(1)}, s32[400]{0:T(512)S(1)}) custom-call(s32[192]{0:T(256)S(1)} %bitcast.8, s32[192]{0:T(256)S(1)} %bitcast.9, s32[2]{0:T(128)S(1)} %pad_add_fusion.scalars, bf16[136,16,128]{2,1,0:T(8,128)(2,1)S(1)} %all_to_all.55.left_own, ...), custom_call_target="tpu_custom_call" | custom-call | flops 1000000000 | bytes 4194304 | tf_op jit(solution)/shard_map/pallas_call | solution.py:296
  27.0 17.7 %all_to_all.56 = f16[264,16,128]{2,1,0:T(8,128)(2,1)S(1)} all-to-all(f16[264,16,128]{2,1,0:T(8,128)(2,1)S(1)} %convert_element_type.42), channel_id=1, replica_groups=mesh['z'=4,'xl'=2,'xh'=2,'y'=4,'c'=2] {'z','xl'}, dimensions={0} | all-to-all | bytes 2162688 | tf_op jit(solution)/shard_map/all_to_all | solution.py:308
  44.9 0.4 shard_map.70
  45.3 15.4 %all_to_all.57.right = bf16[264,16,128]{2,1,0:T(8,128)(2,1)S(1)} all-to-all(bf16[264,16,128]{2,1,0:T(8,128)(2,1)S(1)} %get-tuple-element.25), channel_id=1, replica_groups=mesh['z'=4,'xl'=2,'xh'=2,'y'=4,'c'=2] {'z','xl'}, dimensions={0} | all-to-all | bytes 2162688 | tf_op jit(solution)/shard_map/all_to_all | solution.py:308
  60.7 1.4 shard_map.72
  62.2 4.9 %collective-permute-start.1 = (f16[136,16,128]{2,1,0:T(8,128)(2,1)S(1)}, f16[136,16,128]{2,1,0:T(8,128)(2,1)S(1)}, u32[]{:S(2)}, u32[]{:S(2)}) collective-permute-start(f16[136,16,128]{2,1,0:T(8,128)(2,1)S(1)} %convert_element_type.44), channel_id=1, source_target_pairs={{0,1},{1,0},{2,3},{3,2},{4,5},{5,4},{6,7},{7,6},{8,9},{9,8},{10,11... | collective-permute-start | bytes 1671176 | tf_op jit(solution)/shard_map/ppermute | solution.py:316
  67.1 1.3 shard_map.71.keep
  69.1 16.0 %all_to_all.58 = f16[136,16,128]{2,1,0:T(8,128)(2,1)S(1)} all-to-all(f16[136,16,128]{2,1,0:T(8,128)(2,1)S(1)} %convert_element_type.46), channel_id=1, replica_groups=mesh['z'=4,'xl'=2,'xh'=2,'y'=4,'c'=2] {'xh','y'}, dimensions={0} | all-to-all | bytes 1114112 | tf_op jit(solution)/shard_map/all_to_all | solution.py:308
  85.2 0.3 shard_map.74
  85.6 14.4 %all_to_all.59.left.left_own = bf16[136,16,128]{2,1,0:T(8,128)(2,1)S(1)} all-to-all(bf16[136,16,128]{2,1,0:T(8,128)(2,1)S(1)} %get-tuple-element.29), channel_id=1, replica_groups=mesh['z'=4,'xl'=2,'xh'=2,'y'=4,'c'=2] {'xh','y'}, dimensions={0} | all-to-all | bytes 1114112 | tf_op jit(solution)/shard_map/all_to_all | solution.py:308
  100.0 1.4 shard_map.75.partial_out
  101.3 0.6 collective-permute-done.2.left
  101.9 1.6 shard_map.76
  103.7 14.3 %all_to_all.60 = f16[264,16,128]{2,1,0:T(8,128)(2,1)S(1)} all-to-all(f16[264,16,128]{2,1,0:T(8,128)(2,1)S(1)} %convert_element_type.48), channel_id=1, replica_groups=mesh['z'=4,'xl'=2,'xh'=2,'y'=4,'c'=2] {'z','xl'}, dimensions={0} | all-to-all | bytes 2162688 | tf_op jit(solution)/shard_map/all_to_all | solution.py:308
  118.2 0.4 shard_map.77
  118.6 14.8 %all_to_all.61.right = bf16[264,16,128]{2,1,0:T(8,128)(2,1)S(1)} all-to-all(bf16[264,16,128]{2,1,0:T(8,128)(2,1)S(1)} %get-tuple-element.33), channel_id=1, replica_groups=mesh['z'=4,'xl'=2,'xh'=2,'y'=4,'c'=2] {'z','xl'}, dimensions={0} | all-to-all | bytes 2162688 | tf_op jit(solution)/shard_map/all_to_all | solution.py:308
  133.4 1.4 shard_map.79
  134.9 5.6 %collective-permute-start.3 = (f16[136,16,128]{2,1,0:T(8,128)(2,1)S(1)}, f16[136,16,128]{2,1,0:T(8,128)(2,1)S(1)}, u32[]{:S(2)}, u32[]{:S(2)}) collective-permute-start(f16[136,16,128]{2,1,0:T(8,128)(2,1)S(1)} %convert_element_type.50), channel_id=1, source_target_pairs={{0,1},{1,0},{2,3},{3,2},{4,5},{5,4},{6,7},{7,6},{8,9},{9,8},{10,11... | collective-permute-start | bytes 1671176 | tf_op jit(solution)/shard_map/ppermute | solution.py:316
  140.6 1.3 shard_map.78.keep
  142.6 15.6 %all_to_all.62 = f16[136,16,128]{2,1,0:T(8,128)(2,1)S(1)} all-to-all(f16[136,16,128]{2,1,0:T(8,128)(2,1)S(1)} %convert_element_type.52), channel_id=1, replica_groups=mesh['z'=4,'xl'=2,'xh'=2,'y'=4,'c'=2] {'xh','y'}, dimensions={0} | all-to-all | bytes 1114112 | tf_op jit(solution)/shard_map/all_to_all | solution.py:308
  158.6 14.4 %all_to_all.63.left.left_own = bf16[136,16,128]{2,1,0:T(8,128)(2,1)S(1)} all-to-all(bf16[136,16,128]{2,1,0:T(8,128)(2,1)S(1)} %get-tuple-element.36), channel_id=1, replica_groups=mesh['z'=4,'xl'=2,'xh'=2,'y'=4,'c'=2] {'xh','y'}, dimensions={0} | all-to-all | bytes 1114112 | tf_op jit(solution)/shard_map/all_to_all | solution.py:308
  173.0 1.4 shard_map.82.partial_out
  174.4 0.6 collective-permute-done.4.left
  175.0 1.6 shard_map.83
  176.8 19.8 %all_to_all.64 = f16[264,16,128]{2,1,0:T(8,128)(2,1)S(1)} all-to-all(f16[264,16,128]{2,1,0:T(8,128)(2,1)S(1)} %convert_element_type.54), channel_id=1, replica_groups=mesh['z'=4,'xl'=2,'xh'=2,'y'=4,'c'=2] {'z','xl'}, dimensions={0} | all-to-all | bytes 2162688 | tf_op jit(solution)/shard_map/all_to_all | solution.py:308
  196.7 0.4 shard_map.84
  197.2 1.1 collective-permute-done.5
  198.4 13.9 %all_to_all.65.sums = f32[64,1,128]{2,1,0:T(1,128)S(1)} all-to-all(f32[64,1,128]{2,1,0:T(1,128)S(1)} %broadcast_in_dim.3), channel_id=1, replica_groups=mesh['z'=4,'xl'=2,'xh'=2,'y'=4,'c'=2] {'z','xl','xh','y'}, dimensions={0} | all-to-all | bytes 65536 | tf_op jit(solution)/shard_map/all_to_all | solution.py:308
  212.2 1.4 shard_map.85
  (32 shorter events, 3.3 us)
Async XLA Ops:
  0.6 0.9 copy-start
  1.5 21.0 %copy-start.1 = (s32[1,1,192]{2,1,0:T(1,128)S(1)}, s32[1,1,192]{2,1,0:T(1,128)}, u32[]{:S(2)}) copy-start(s32[1,1,192]{2,1,0:T(1,128)} %param.6) | copy-start | bytes 2308
  1.5 21.0 %copy-start.2 = (s32[1,1,192]{2,1,0:T(1,128)S(1)}, s32[1,1,192]{2,1,0:T(1,128)}, u32[]{:S(2)}) copy-start(s32[1,1,192]{2,1,0:T(1,128)} %param.7) | copy-start | bytes 2308
  20.6 2.0 collective-permute-start
  62.2 6.5 %collective-permute-start.1 = (f16[136,16,128]{2,1,0:T(8,128)(2,1)S(1)}, f16[136,16,128]{2,1,0:T(8,128)(2,1)S(1)}, u32[]{:S(2)}, u32[]{:S(2)}) collective-permute-start(f16[136,16,128]{2,1,0:T(8,128)(2,1)S(1)} %convert_element_type.44), channel_id=1, source_target_pairs={{0,1},{1,0},{2,3},{3,2},{4,5},{5,4},{6,7},{7,6},{8,9},{9,8},{10,11... | collective-permute-start | bytes 1671176 | tf_op jit(solution)/shard_map/ppermute | solution.py:316
  100.0 2.0 collective-permute-start.2
  134.9 7.2 %collective-permute-start.3 = (f16[136,16,128]{2,1,0:T(8,128)(2,1)S(1)}, f16[136,16,128]{2,1,0:T(8,128)(2,1)S(1)}, u32[]{:S(2)}, u32[]{:S(2)}) collective-permute-start(f16[136,16,128]{2,1,0:T(8,128)(2,1)S(1)} %convert_element_type.50), channel_id=1, source_target_pairs={{0,1},{1,0},{2,3},{3,2},{4,5},{5,4},{6,7},{7,6},{8,9},{9,8},{10,11... | collective-permute-start | bytes 1671176 | tf_op jit(solution)/shard_map/ppermute | solution.py:316
  173.0 2.0 collective-permute-start.4
  197.2 1.2 collective-permute-start.5

commit v5 on v4

--- a/solution.py
+++ b/solution.py
@@ -15,7 +15,7 @@
 SLOTS = 192
 COUNTS = 2 * SLOTS
 FIRST_CHUNK = 32
-LIST_CHUNK = 32
+LIST_CHUNK = 64
 STAGGER = 7000
 CHIPS_OF_COL = ("xh", "y")
 DEVICES_OF_ROW = ("z", "xl")

time: 214 us -> 215 us (level)
  Pallas kernels: 19.8 us -> 24.3 us
    pallas_call x9, Pallas kernels: 15.7 us -> 20.2 us  [kernel_call(): pl.pallas_call(body, out_shape=outs, in_specs=specs, out_specs=[pl.BlockS...]
  transfers between devices with their start and end apart: 6 -> 6, of which waited for: 6 -> 4; matrix products, arithmetic and copies ran while one was open for 0% -> 0% of each run, Pallas kernels for 2% -> 3%
where the time goes in v5:
time: 215 us
  blocking collectives  175 us (81%)
  Pallas kernels  24.3 us (11%)
  starting transfers between devices  9.62 us (4%)
  waiting for transfers between devices  2.58 us (1%)
    all_to_all x11, blocking collectives, exchange(): return lax.all_to_all(sent, axes, 0, 0, tiled=True)  175 us
    pallas_call x9, Pallas kernels, kernel_call(): pl.pallas_call(body, out_shape=outs, in_specs=specs, out_specs=[pl.BlockS...  20.2 us
    ppermute x6, starting transfers between devices, swap_cores(): return lax.ppermute(values, 'c', [(0, 1), (1, 0)])  9.62 us
  transfers between devices with their start and end apart: 6, of which 4 were waited for; matrix products, arithmetic and copies ran while one was open for 0% of the time, Pallas kernels for 3%

profile of v5, /device:TPU:0, one launch (start us, length us, event | category | flops | bytes accessed | tf_op | source)
XLA Modules:
  0.0 215.1 jit_solution(2836508468090666984)
XLA Ops:
  0.6 0.9 copy-done
  1.6 19.0 %all_to_all.55.left_own = bf16[136,16,128]{2,1,0:T(8,128)(2,1)S(1)} all-to-all(bf16[136,16,128]{2,1,0:T(8,128)(2,1)S(1)} %get-tuple-element.22), channel_id=1, replica_groups=mesh['z'=4,'xl'=2,'xh'=2,'y'=4,'c'=2] {'xh','y'}, dimensions={0} | all-to-all | bytes 1114112 | tf_op jit(solution)/shard_map/all_to_all | solution.py:308
  21.3 1.2 collective-permute-done.left_other
  22.6 4.6 %shard_map.69 = (f32[264,16,128]{2,1,0:T(8,128)S(1)}, bf16[192,128,128]{2,1,0:T(8,128)(2,1)S(1)}, bf16[192,128,128]{2,1,0:T(8,128)(2,1)S(1)}, s32[400]{0:T(512)S(1)}) custom-call(s32[192]{0:T(256)S(1)} %bitcast.8, s32[192]{0:T(256)S(1)} %bitcast.9, s32[2]{0:T(128)S(1)} %pad_add_fusion.scalars, bf16[136,16,128]{2,1,0:T(8,128)(2,1)S(1)} %all_to_all.55.left_own, ...), custom_call_target="tpu_custom_call" | custom-call | flops 1000000000 | bytes 4194304 | tf_op jit(solution)/shard_map/pallas_call | solution.py:296
  27.3 16.8 %all_to_all.56 = f16[264,16,128]{2,1,0:T(8,128)(2,1)S(1)} all-to-all(f16[264,16,128]{2,1,0:T(8,128)(2,1)S(1)} %convert_element_type.42), channel_id=1, replica_groups=mesh['z'=4,'xl'=2,'xh'=2,'y'=4,'c'=2] {'z','xl'}, dimensions={0} | all-to-all | bytes 2162688 | tf_op jit(solution)/shard_map/all_to_all | solution.py:308
  44.4 0.4 shard_map.70
  44.8 15.5 %all_to_all.57.right = bf16[264,16,128]{2,1,0:T(8,128)(2,1)S(1)} all-to-all(bf16[264,16,128]{2,1,0:T(8,128)(2,1)S(1)} %get-tuple-element.25), channel_id=1, replica_groups=mesh['z'=4,'xl'=2,'xh'=2,'y'=4,'c'=2] {'z','xl'}, dimensions={0} | all-to-all | bytes 2162688 | tf_op jit(solution)/shard_map/all_to_all | solution.py:308
  60.3 1.9 shard_map.72
  62.3 4.6 %collective-permute-start.1 = (f16[136,16,128]{2,1,0:T(8,128)(2,1)S(1)}, f16[136,16,128]{2,1,0:T(8,128)(2,1)S(1)}, u32[]{:S(2)}, u32[]{:S(2)}) collective-permute-start(f16[136,16,128]{2,1,0:T(8,128)(2,1)S(1)} %convert_element_type.44), channel_id=1, source_target_pairs={{0,1},{1,0},{2,3},{3,2},{4,5},{5,4},{6,7},{7,6},{8,9},{9,8},{10,11... | collective-permute-start | bytes 1671176 | tf_op jit(solution)/shard_map/ppermute | solution.py:316
  66.9 1.8 shard_map.71.keep
  69.2 16.2 %all_to_all.58 = f16[136,16,128]{2,1,0:T(8,128)(2,1)S(1)} all-to-all(f16[136,16,128]{2,1,0:T(8,128)(2,1)S(1)} %convert_element_type.46), channel_id=1, replica_groups=mesh['z'=4,'xl'=2,'xh'=2,'y'=4,'c'=2] {'xh','y'}, dimensions={0} | all-to-all | bytes 1114112 | tf_op jit(solution)/shard_map/all_to_all | solution.py:308
  85.4 0.3 shard_map.74
  85.8 14.5 %all_to_all.59.left.left_own = bf16[136,16,128]{2,1,0:T(8,128)(2,1)S(1)} all-to-all(bf16[136,16,128]{2,1,0:T(8,128)(2,1)S(1)} %get-tuple-element.29), channel_id=1, replica_groups=mesh['z'=4,'xl'=2,'xh'=2,'y'=4,'c'=2] {'xh','y'}, dimensions={0} | all-to-all | bytes 1114112 | tf_op jit(solution)/shard_map/all_to_all | solution.py:308
  100.3 1.9 shard_map.75.partial_out
  102.2 2.2 %shard_map.76 = f32[264,16,128]{2,1,0:T(8,128)S(1)} custom-call(s32[400]{0:T(512)S(1)} %get-tuple-element.23.table, bf16[136,16,128]{2,1,0:T(8,128)(2,1)S(1)} %all_to_all.59.left.left_own, bf16[136,16,128]{2,1,0:T(8,128)(2,1)S(1)} %collective-permute-done.2.left, f32[264,16,128]{2,1,0:T(8,128)S(1)} %shard_map.75.partial_out, ...), custom_call_target="tpu_custom_call" | custom-call | flops 1000000000 | bytes 4194304 | tf_op jit(solution)/shard_map/pallas_call | solution.py:296
  104.5 14.3 %all_to_all.60 = f16[264,16,128]{2,1,0:T(8,128)(2,1)S(1)} all-to-all(f16[264,16,128]{2,1,0:T(8,128)(2,1)S(1)} %convert_element_type.48), channel_id=1, replica_groups=mesh['z'=4,'xl'=2,'xh'=2,'y'=4,'c'=2] {'z','xl'}, dimensions={0} | all-to-all | bytes 2162688 | tf_op jit(solution)/shard_map/all_to_all | solution.py:308
  119.0 0.4 shard_map.77
  119.4 15.1 %all_to_all.61.right = bf16[264,16,128]{2,1,0:T(8,128)(2,1)S(1)} all-to-all(bf16[264,16,128]{2,1,0:T(8,128)(2,1)S(1)} %get-tuple-element.33), channel_id=1, replica_groups=mesh['z'=4,'xl'=2,'xh'=2,'y'=4,'c'=2] {'z','xl'}, dimensions={0} | all-to-all | bytes 2162688 | tf_op jit(solution)/shard_map/all_to_all | solution.py:308
  134.5 1.9 shard_map.79
  136.6 5.0 %collective-permute-start.3 = (f16[136,16,128]{2,1,0:T(8,128)(2,1)S(1)}, f16[136,16,128]{2,1,0:T(8,128)(2,1)S(1)}, u32[]{:S(2)}, u32[]{:S(2)}) collective-permute-start(f16[136,16,128]{2,1,0:T(8,128)(2,1)S(1)} %convert_element_type.50), channel_id=1, source_target_pairs={{0,1},{1,0},{2,3},{3,2},{4,5},{5,4},{6,7},{7,6},{8,9},{9,8},{10,11... | collective-permute-start | bytes 1671176 | tf_op jit(solution)/shard_map/ppermute | solution.py:316
  141.6 1.8 shard_map.78.keep
  143.5 0.3 shard_map.80
  143.8 15.1 %all_to_all.62 = f16[136,16,128]{2,1,0:T(8,128)(2,1)S(1)} all-to-all(f16[136,16,128]{2,1,0:T(8,128)(2,1)S(1)} %convert_element_type.52), channel_id=1, replica_groups=mesh['z'=4,'xl'=2,'xh'=2,'y'=4,'c'=2] {'xh','y'}, dimensions={0} | all-to-all | bytes 1114112 | tf_op jit(solution)/shard_map/all_to_all | solution.py:308
  159.0 0.3 shard_map.81
  159.4 14.6 %all_to_all.63.left.left_own = bf16[136,16,128]{2,1,0:T(8,128)(2,1)S(1)} all-to-all(bf16[136,16,128]{2,1,0:T(8,128)(2,1)S(1)} %get-tuple-element.36), channel_id=1, replica_groups=mesh['z'=4,'xl'=2,'xh'=2,'y'=4,'c'=2] {'xh','y'}, dimensions={0} | all-to-all | bytes 1114112 | tf_op jit(solution)/shard_map/all_to_all | solution.py:308
  174.0 1.9 shard_map.82.partial_out
  175.9 2.3 %shard_map.83 = f32[264,16,128]{2,1,0:T(8,128)S(1)} custom-call(s32[400]{0:T(512)S(1)} %get-tuple-element.23.table, bf16[136,16,128]{2,1,0:T(8,128)(2,1)S(1)} %all_to_all.63.left.left_own, bf16[136,16,128]{2,1,0:T(8,128)(2,1)S(1)} %collective-permute-done.4.left, f32[264,16,128]{2,1,0:T(8,128)S(1)} %shard_map.82.partial_out, ...), custom_call_target="tpu_custom_call" | custom-call | flops 1000000000 | bytes 4194304 | tf_op jit(solution)/shard_map/pallas_call | solution.py:296
  178.4 19.5 %all_to_all.64 = f16[264,16,128]{2,1,0:T(8,128)(2,1)S(1)} all-to-all(f16[264,16,128]{2,1,0:T(8,128)(2,1)S(1)} %convert_element_type.54), channel_id=1, replica_groups=mesh['z'=4,'xl'=2,'xh'=2,'y'=4,'c'=2] {'z','xl'}, dimensions={0} | all-to-all | bytes 2162688 | tf_op jit(solution)/shard_map/all_to_all | solution.py:308
  198.1 0.4 shard_map.84
  198.5 1.1 collective-permute-done.5
  199.7 14.0 %all_to_all.65.sums = f32[64,1,128]{2,1,0:T(1,128)S(1)} all-to-all(f32[64,1,128]{2,1,0:T(1,128)S(1)} %broadcast_in_dim.3), channel_id=1, replica_groups=mesh['z'=4,'xl'=2,'xh'=2,'y'=4,'c'=2] {'z','xl','xh','y'}, dimensions={0} | all-to-all | bytes 65536 | tf_op jit(solution)/shard_map/all_to_all | solution.py:308
  213.7 1.4 shard_map.85
  (32 shorter events, 2.3 us)
Async XLA Ops:
  0.6 0.9 copy-start
  1.5 21.0 %copy-start.1 = (s32[1,1,192]{2,1,0:T(1,128)S(1)}, s32[1,1,192]{2,1,0:T(1,128)}, u32[]{:S(2)}) copy-start(s32[1,1,192]{2,1,0:T(1,128)} %param.6) | copy-start | bytes 2308
  1.5 21.0 %copy-start.2 = (s32[1,1,192]{2,1,0:T(1,128)S(1)}, s32[1,1,192]{2,1,0:T(1,128)}, u32[]{:S(2)}) copy-start(s32[1,1,192]{2,1,0:T(1,128)} %param.7) | copy-start | bytes 2308
  20.6 2.0 collective-permute-start
  62.3 6.4 %collective-permute-start.1 = (f16[136,16,128]{2,1,0:T(8,128)(2,1)S(1)}, f16[136,16,128]{2,1,0:T(8,128)(2,1)S(1)}, u32[]{:S(2)}, u32[]{:S(2)}) collective-permute-start(f16[136,16,128]{2,1,0:T(8,128)(2,1)S(1)} %convert_element_type.44), channel_id=1, source_target_pairs={{0,1},{1,0},{2,3},{3,2},{4,5},{5,4},{6,7},{7,6},{8,9},{9,8},{10,11... | collective-permute-start | bytes 1671176 | tf_op jit(solution)/shard_map/ppermute | solution.py:316
  100.3 2.0 collective-permute-start.2
  136.6 6.8 %collective-permute-start.3 = (f16[136,16,128]{2,1,0:T(8,128)(2,1)S(1)}, f16[136,16,128]{2,1,0:T(8,128)(2,1)S(1)}, u32[]{:S(2)}, u32[]{:S(2)}) collective-permute-start(f16[136,16,128]{2,1,0:T(8,128)(2,1)S(1)} %convert_element_type.50), channel_id=1, source_target_pairs={{0,1},{1,0},{2,3},{3,2},{4,5},{5,4},{6,7},{7,6},{8,9},{9,8},{10,11... | collective-permute-start | bytes 1671176 | tf_op jit(solution)/shard_map/ppermute | solution.py:316
  173.9 2.0 collective-permute-start.4
  198.5 1.2 collective-permute-start.5
